TPU v7x, 128 devices: a whole 4x4x4 slice. The times are simulated.
128 devices in a mesh: ia: 8 (over y, core), ja: 16 (over x, z).
Axes of the slice: x: 4, y: 4, z: 4, core: 2. Of those that a mesh axis runs over, the one named last changes fastest.
Arguments:
- amplitudes: bfloat16 [1024, 128, 128], P(('ia', 'ja')), may hold values from -6 to 6
- bases: bfloat16 [1024, 512, 128], P(('ia', 'ja')), may hold values from -1 to 1
- exchange_ints: bfloat16 [1024, 128, 128], P(('ia', 'ja')), may hold values from -6 to 6
- cycle_ints: bfloat16 [1024, 32, 128, 128], P(('ia', 'ja')), may hold values from -0.0625 to 0.0625
- pno_energy: float32 [1024, 128], P(('ia', 'ja')), may hold values from 0.2 to 3
- occ_energy: float32 [1024], P(('ia', 'ja')), may hold values from -1.5 to -0.3
- pno_count: int32 [1024], P(('ia', 'ja')), may hold values from 32 to 128, as said below
- coupling: int32 [1024, 32], P(('ia', 'ja')), may hold values from 0 to 1023, as said below
- reverse: int32 [1024], P(('ia', 'ja')), may hold values from 0 to 1023, as said below
Outputs:
- new_amplitudes: bfloat16 [1024, 128, 128], P(('ia', 'ja'))
- residual: float32 [1024, 128, 128], P(('ia', 'ja'))
Inputs may be any that keep to these rules, and one draw needn't show every extreme that they name: `coupling`: pair p is owned by the device at linear index p // 8 of the mesh (ia slowest). Over the 8 pairs of one device, the lists have exactly 2 entries that name pairs of each device (the device itself included), and these name exactly 1 distinct pairs of that device. `reverse`: reversal is an involution without fixed points; the reversed pair of a pair owned by the device at ja index b lies on the device with the same ia index and ja index b + 8 modulo 2 * 8. `pno_count`: some pair keeps all 128 natural orbitals.
All inputs are finite; a program needn't handle non-finite values.
Results may differ from a plain program's by a relative error of at most 0.0061.
Values may be sent and summed in bfloat16 or wider, within the bound.
No kernel may reach another device: no remote copies, remote signals or barrier semaphores. Data moves between devices by JAX's collectives and lax.ppermute only.
A program may use at most 192 MiB of HBM per device.

v0:
```python
import functools

import jax
import jax.numpy as jnp
from jax import lax
from jax.experimental import pallas as pl
from jax.experimental.pallas import tpu as pltpu
from jax.sharding import PartitionSpec as P


RING = 4
AXES = ("ia", "ja")
CHUNKS = (
    ((0, 0), (0, 1), (0, 3), (3, 0)),
    ((1, 0), (3, 3), (1, 1), (3, 1)),
    ((1, 3), (0, 2), (3, 2), (1, 2)),
    ((2, 0), (2, 1), (2, 2), (2, 3)),
)
NOTES = 16
NT = (((1,), (1,)), ((), ()))


def ring_perm(stage, shift):
    pairs = []
    for i in range(2 * RING):
        for x in range(RING):
            for z in range(RING):
                if (i % 2 == 0) == (stage == 1):
                    there = (x + shift) % RING * RING + z
                else:
                    there = x * RING + (z + shift) % RING
                pairs.append((i * RING * RING + x * RING + z, i * RING * RING + there))
    return pairs


def shift_ja(value, stage, shift):
    return lax.ppermute(value, AXES, ring_perm(stage, shift))


def shift_ia(value, steps, flip):
    size = 2 * RING
    return lax.ppermute(
        value, "ia", [(i, (i // 2 + steps) % RING * 2 + (i % 2 ^ flip)) for i in range(size)]
    )


def owner_ja(core, x, z, u, t):
    dx = jnp.where(core == 0, t, u)
    dz = jnp.where(core == 0, u, t)
    return ((x + dx) & 3) * RING + ((z + dz) & 3)


def transform_kernel(chunk, starts, codes, me, *refs):
    blocks, lines = refs[:4], refs[4 : 4 + len(starts)]
    refs = refs[4 + len(starts) :]
    targets = refs[:8]
    owned, line_buf, result, own_sems, line_sems, out_sems = refs[8:]
    width = result.shape[-1]
    depth = owned.shape[2] - width
    rows = line_buf.shape[2]
    i, j = me[0], me[1]
    core, x, z = i & 1, j >> 2, j & 3

    def own(n):
        return pltpu.make_async_copy(blocks[n], owned.at[n], own_sems.at[n])

    def fetch(k, part, slot):
        source = lines[2 * k + part]
        return pltpu.make_async_copy(
            source.at[pl.ds(starts[2 * k + part], rows)],
            line_buf.at[slot, part],
            line_sems.at[slot, part],
        )

    def emit(k, slot):
        return pltpu.make_async_copy(result.at[slot], targets[k], out_sems.at[slot])

    for part in range(2):
        fetch(0, part, 0).start()
    for n in range(len(chunk)):
        own(n).start()
    for n in range(len(chunk)):
        own(n).wait()

    def reader(r, carry):
        slot = r & 1
        for k in range(1, 8):

            @pl.when(r + 1 == k)
            def _():
                for part in range(2):
                    fetch(k, part, k & 1).start()

        for part in range(2):
            fetch(0, part, slot).wait()

        @pl.when(r >= 2)
        def _():
            emit(0, slot).wait()

        inter, proj = [], []
        for n, (u, t) in enumerate(chunk):
            code = codes[r, i * 16 + owner_ja(core, x, z, u, t)]
            q = code & 7
            first, second = (code >> 3) & 7, code >> 6
            mine = jnp.concatenate(
                [
                    line_buf[slot, at >> 2, pl.ds(pl.multiple_of((at & 3) * width, width), width)]
                    for at in (first, second)
                ],
                axis=0,
            )
            inter.append(
                (
                    q,
                    jnp.dot(
                        mine, owned[n, q, :depth], preferred_element_type=jnp.float32
                    ).astype(jnp.bfloat16),
                )
            )
        for n, (q, value) in enumerate(inter):
            proj.append(
                jnp.dot(
                    value, owned[n, q, depth:], preferred_element_type=jnp.float32
                ).astype(jnp.bfloat16)
            )
        for n, (q, value) in enumerate(inter):
            for h in range(2):
                side = slice(h * width, (h + 1) * width)
                result[slot, n, h] = lax.dot_general(
                    proj[n][side], value[side], NT, preferred_element_type=jnp.float32
                ).astype(jnp.bfloat16)
        for k in range(8):

            @pl.when(r == k)
            def _():
                emit(k, k & 1).start()

        return carry

    lax.fori_loop(0, 8, reader, 0)
    for slot in range(2):
        emit(0, slot).wait()


def transform(chunk, codes, me, blocks, lines):
    pairs, rows, width = blocks[0].shape
    depth = rows - width
    smem = pl.BlockSpec(memory_space=pltpu.SMEM)
    hbm = pl.BlockSpec(memory_space=pltpu.HBM)
    shape = (len(chunk), 2, width, width)
    one = jax.ShapeDtypeStruct(shape, jnp.bfloat16)
    flops = 64 * 2 * width * width * (depth + 2 * width)
    return pl.pallas_call(
        functools.partial(transform_kernel, chunk, tuple(start for _, start in lines)),
        out_shape=[one] * 8,
        in_specs=[smem, smem] + [hbm] * (4 + len(lines)),
        out_specs=[hbm] * 8,
        scratch_shapes=[
            pltpu.VMEM((len(chunk),) + blocks[0].shape, jnp.bfloat16),
            pltpu.VMEM((2, 2, pairs // 2 * width, depth), jnp.bfloat16),
            pltpu.VMEM((2,) + shape, jnp.bfloat16),
            pltpu.SemaphoreType.DMA((len(chunk),)),
            pltpu.SemaphoreType.DMA((2, 2)),
            pltpu.SemaphoreType.DMA((2,)),
        ],
        compiler_params=pltpu.CompilerParams(vmem_limit_bytes=24 << 20),
        cost_estimate=pl.CostEstimate(
            flops=4 * flops, bytes_accessed=16 << 20, transcendentals=0
        ),
        name="transform",
    )(codes, me, *blocks, *[line for line, _ in lines])


def cycle_kernel(chunk, spots, me, cycle, *refs):
    arrived, before, total = refs[:8], refs[8], refs[9]
    values, sums, sems = refs[10:]
    i, j = me[0], me[1]
    y, core = i >> 1, i & 1
    x, z = j >> 2, j & 3

    copies = [
        pltpu.make_async_copy(arrived[r], values.at[r], sems.at[r]) for r in range(8)
    ]
    for copy in copies:
        copy.start()
    sums[...] = before[...]
    for r in range(8):
        other = core ^ (r >> 2)
        worker = ((y - (r & 3)) & 3) * 2 + other
        copies[r].wait()
        parts = []
        for n, (u, t) in enumerate(chunk):
            owner = worker * 16 + owner_ja(other, x, z, u, t)
            for h in range(2):
                spot = spots[h * 128 + owner]
                block = cycle[spot]
                value = values[r, n, h]
                part = jnp.dot(block, value, preferred_element_type=jnp.float32)
                part += lax.dot_general(value, block, NT, preferred_element_type=jnp.float32)
                parts.append((spot >> 5, part))
        for place, part in parts:
            sums[place] += part
    total[...] = sums[...].astype(total.dtype)


def cycle_part(chunk, spots, me, cycle, arrived, before, dtype):
    smem = pl.BlockSpec(memory_space=pltpu.SMEM)
    vmem = pl.BlockSpec(memory_space=pltpu.VMEM)
    hbm = pl.BlockSpec(memory_space=pltpu.HBM)
    width = cycle.shape[-1]
    return pl.pallas_call(
        functools.partial(cycle_kernel, chunk),
        out_shape=jax.ShapeDtypeStruct(before.shape, dtype),
        in_specs=[smem, smem, vmem] + [hbm] * 8 + [vmem],
        out_specs=vmem,
        scratch_shapes=[
            pltpu.VMEM((8,) + arrived[0].shape, jnp.bfloat16),
            pltpu.VMEM(before.shape, jnp.float32),
            pltpu.SemaphoreType.DMA((8,)),
        ],
        compiler_params=pltpu.CompilerParams(vmem_limit_bytes=20 << 20),
        cost_estimate=pl.CostEstimate(
            flops=4 * 64 * 4 * width**3, bytes_accessed=6 << 20, transcendentals=0
        ),
        name="cycle",
    )(spots, me, cycle, *arrived, before)


def prep_kernel(count, entries, amps, bases, block, line, masked, spots):
    p = pl.program_id(0)
    depth, width = bases.shape[1], bases.shape[2]
    pairs = pl.num_programs(0)
    cols = count[p]
    lane = lax.broadcasted_iota(jnp.int32, (depth, width), 1) < cols
    kept = jnp.where(lane, bases[0], jnp.zeros_like(bases[0]))
    block[0, :depth] = kept
    square = lane[:width] & (lax.broadcasted_iota(jnp.int32, (width, width), 0) < cols)
    kept_amps = jnp.where(square, amps[0], jnp.zeros_like(amps[0]))
    block[0, depth:] = kept_amps
    masked[0] = kept_amps
    line[pl.ds(pl.multiple_of(p * width, width), width)] = kept.T

    @pl.when(p == 0)
    def _():
        number = entries.shape[1]
        devices = spots.shape[1]
        row = jnp.broadcast_to(entries[...], (number, number))
        down = row.T
        at = lax.broadcasted_iota(jnp.int32, (number, number), 0)
        before = lax.broadcasted_iota(jnp.int32, (number, number), 1)
        same = ((row >> 3) == (down >> 3)) & (before < at)
        later = jnp.sum(same.astype(jnp.int32), axis=1, keepdims=True)
        named = (down[:, :devices] >> 3) == before[:, :devices]
        head = named & (later == 0)
        tail = named & (later == 1)
        place = at[:, :devices]
        zero = jnp.zeros_like(place)
        spot_head = jnp.sum(jnp.where(head, place, zero), axis=0, keepdims=True)
        spot_tail = jnp.sum(jnp.where(tail, place, zero), axis=0, keepdims=True)
        which = jnp.sum(jnp.where(head, down[:, :devices] & 7, zero), axis=0, keepdims=True)
        spots[0:1] = spot_head
        spots[1:2] = spot_tail
        row = lax.broadcasted_iota(jnp.int32, (NOTES, devices), 0)
        notes = jnp.where(row == 0, which, jnp.where(row == 1, spot_head >> 5, spot_tail >> 5))
        line[pl.ds(pairs * width, NOTES), :devices] = notes.astype(jnp.float32).astype(
            jnp.bfloat16
        )
        line[pl.ds(pairs * width, NOTES), devices:] = jnp.zeros(
            (NOTES, depth - devices), jnp.bfloat16
        )


def prep(count, entries, amps, bases):
    pairs, depth, width = bases.shape
    devices = entries.shape[1] // 2
    smem = pl.BlockSpec(memory_space=pltpu.SMEM)
    each = lambda *shape: pl.BlockSpec((1,) + shape, lambda p: (p, 0, 0))
    whole = lambda *shape: pl.BlockSpec(shape, lambda p: (0,) * len(shape))
    bf16 = jnp.bfloat16
    return pl.pallas_call(
        prep_kernel,
        grid=(pairs,),
        out_shape=(
            jax.ShapeDtypeStruct((pairs, depth + width, width), bf16),
            jax.ShapeDtypeStruct((pairs * width + NOTES, depth), bf16),
            jax.ShapeDtypeStruct(amps.shape, bf16),
            jax.ShapeDtypeStruct((2, devices), jnp.int32),
        ),
        in_specs=[smem, whole(1, 2 * devices), each(width, width), each(depth, width)],
        out_specs=(
            each(depth + width, width),
            whole(pairs * width + NOTES, depth),
            each(width, width),
            whole(2, devices),
        ),
        compiler_params=pltpu.CompilerParams(vmem_limit_bytes=16 << 20),
        cost_estimate=pl.CostEstimate(flops=0, bytes_accessed=5 << 20, transcendentals=0),
        name="prep",
    )(
        count,
        entries,
        pltpu.with_memory_space_constraint(amps, pltpu.HBM),
        pltpu.with_memory_space_constraint(bases, pltpu.HBM),
    )


def notes_kernel(ends, *refs):
    sources, codes, notes, sems = refs[:8], *refs[8:]
    devices = codes.shape[1]
    copies = [
        pltpu.make_async_copy(
            sources[r].at[pl.ds(ends[r], NOTES), pl.ds(0, devices)], notes.at[r], sems.at[r]
        )
        for r in range(8)
    ]
    for copy in copies:
        copy.start()
    for r in range(8):
        copies[r].wait()
        values = notes[r].astype(jnp.float32).astype(jnp.int32)
        codes[r : r + 1] = values[0:1] + 8 * values[1:2] + 64 * values[2:3]


def read_notes(lines, devices):
    hbm = pl.BlockSpec(memory_space=pltpu.HBM)
    ends = tuple(value.shape[0] - NOTES for value in lines)
    return pl.pallas_call(
        functools.partial(notes_kernel, ends),
        out_shape=jax.ShapeDtypeStruct((8, devices), jnp.int32),
        in_specs=[hbm] * 8,
        out_specs=pl.BlockSpec(memory_space=pltpu.VMEM),
        scratch_shapes=[
            pltpu.VMEM((8, NOTES, devices), jnp.bfloat16),
            pltpu.SemaphoreType.DMA((8,)),
        ],
        name="notes",
    )(*lines)


def finish_kernel(rev, count, occ, exchange, amps, own, partner, energy, new, res):
    pairs, width = amps.shape[0], amps.shape[1]
    row = lax.broadcasted_iota(jnp.int32, (width, width), 0)
    col = lax.broadcasted_iota(jnp.int32, (width, width), 1)
    for p in range(pairs):
        keep = (row < count[p]) & (col < count[p])
        mirrored = partner[rev[p]].astype(jnp.float32).T
        total = exchange[p].astype(jnp.float32) + own[p].astype(jnp.float32) + mirrored
        total = jnp.where(keep, total, 0.0)
        across = jnp.broadcast_to(energy[pl.ds(p, 1), :], (width, width))
        below = across.T + across - occ[p]
        res[p] = total
        updated = amps[p].astype(jnp.float32) - total / below
        new[p] = jnp.where(keep, updated, 0.0).astype(jnp.bfloat16)


def finish(rev, count, occ, exchange, amps, own, partner, energy):
    smem = pl.BlockSpec(memory_space=pltpu.SMEM)
    vmem = pl.BlockSpec(memory_space=pltpu.VMEM)
    return pl.pallas_call(
        finish_kernel,
        out_shape=(
            jax.ShapeDtypeStruct(amps.shape, jnp.bfloat16),
            jax.ShapeDtypeStruct(amps.shape, jnp.float32),
        ),
        in_specs=[smem] * 3 + [vmem] * 5,
        out_specs=(vmem, vmem),
        name="finish",
    )(rev, count, occ, exchange, amps, own, partner, energy)


def update(
    amplitudes,
    bases,
    exchange_ints,
    cycle_ints,
    pno_energy,
    occ_energy,
    pno_count,
    coupling,
    reverse,
):
    pairs, width = amplitudes.shape[0], amplitudes.shape[1]
    couple = coupling.shape[1]
    me = jnp.stack([lax.axis_index("ia"), lax.axis_index("ja")]).astype(jnp.int32)
    block, line, amps_masked, spots = prep(
        pno_count, coupling.reshape(1, -1), amplitudes, bases
    )
    devices = spots.shape[1]
    spots = spots.reshape(-1)
    half = line.shape[0] // 2 // width * width

    below = shift_ia(line, 1, 0)
    above = shift_ia(line, -1, 0)

    first = {0: block}
    first[3] = shift_ja(block, 1, 1)
    first[1] = shift_ja(block, 1, -1)
    held = {}
    held[3, 0] = shift_ja(block, 2, 1)
    held[1, 0] = shift_ja(block, 2, -1)

    far_a = shift_ia(below[:half], 1, 0)
    far_b = shift_ia(above[half:], -1, 0)
    block, first[1], first[3] = lax.optimization_barrier((block, first[1], first[3]))
    for t in (3, 1):
        held[3, t] = shift_ja(first[t], 2, 1)
    for t in (1, 3):
        held[1, t] = shift_ja(first[t], 2, -1)
    first[2] = shift_ja(block, 1, 2)
    near = []
    for value in (line, above, below):
        near.append(shift_ia(value, 0, 1))
    far = []
    for value in (far_a, far_b):
        far.append(shift_ia(value, 0, 1))

    def halves(value):
        return [(value, 0), (value, half)]

    lines = halves(line) + halves(above) + [(far_a, 0), (far_b, 0)] + halves(below)
    lines += halves(near[0]) + halves(near[1]) + [(far[0], 0), (far[1], 0)] + halves(near[2])
    codes = read_notes([lines[2 * r + 1][0] for r in range(8)], devices)
    for t in (0, 1, 3):
        held[0, t] = first[t]

    cycle = pltpu.with_memory_space_constraint(
        cycle_ints.reshape(pairs * couple, width, width), pltpu.VMEM
    )
    total = jnp.zeros((pairs, width, width), jnp.float32)
    arrivals = []
    for c, chunk in enumerate(CHUNKS):
        if c >= 2:
            total = cycle_part(
                CHUNKS[c - 2], spots, me, cycle, arrivals[c - 2], total, jnp.float32
            )
            codes, total = lax.optimization_barrier((codes, total))
        sent = transform(chunk, codes, me, [held[key] for key in chunk], lines)
        sent, total = lax.optimization_barrier((sent, total))
        if c == 0:
            held[0, 2] = first[2]
            for u, shift in ((3, 1), (1, -1)):
                held[u, 2] = shift_ja(first[2], 2, shift)
            for u, t, shift in ((3, 0, 1), (1, 1, -1), (3, 3, 1)):
                held[2, t] = shift_ja(held[u, t], 2, shift)
            held[2, 2] = shift_ja(first[2], 2, 2)
        back = [sent[0]]
        for r in range(1, 8):
            back.append(shift_ia(sent[r], r & 3, r >> 2))
        arrivals.append(back)
    total = cycle_part(CHUNKS[2], spots, me, cycle, arrivals[2], total, jnp.float32)
    cycle_sum = cycle_part(CHUNKS[3], spots, me, cycle, arrivals[3], total, jnp.bfloat16)
    apart = lax.axis_size("ja") // 2
    partner = lax.ppermute(cycle_sum, "ja", [(b, b ^ apart) for b in range(2 * apart)])
    return finish(
        reverse % pairs,
        pno_count,
        occ_energy,
        exchange_ints,
        amps_masked,
        cycle_sum,
        partner,
        pno_energy,
    )


def solution(mesh):
    return jax.shard_map(
        update,
        mesh=mesh,
        in_specs=(
            P(AXES, None, None),
            P(AXES, None, None),
            P(AXES, None, None),
            P(AXES, None, None, None),
            P(AXES, None),
            P(AXES),
            P(AXES),
            P(AXES, None),
            P(AXES),
        ),
        out_specs=(P(AXES, None, None), P(AXES, None, None)),
        check_vma=False,
    )
```

profile of v0, /device:TPU:1, one launch (start us, length us, event | category | flops | bytes accessed | tf_op | source)
XLA Modules:
  0.0 270.7 jit_solution(11920928482944492611)
XLA Ops:
  2.1 5.9 %prep.1 = (bf16[8,640,128]{2,1,0:T(8,128)(2,1)}, bf16[1040,512]{1,0:T(8,128)(2,1)S(1)}, bf16[8,128,128]{2,1,0:T(8,128)(2,1)S(1)}, s32[2,128]{1,0:T(2,128)S(1)}) custom-call(s32[8]{0:T(128)S(1)} %copy-done.19, s32[1,256]{1,0:T(1,128)S(1)} %reshape.13.entries, bf16[8,128,128]{2,1,0:T(8,128)(2,1)} %amps.1, bf16[8,512,128]{2,1,0:T(8,128)(2,1)} %bases.1), custom_call_target="tpu_custom_call" | custom-call | bytes 5242880 | tf_op jit(solution)/shard_map/prep/pallas_call | solution.py:281
  8.7 3.6 %collective-permute-start = (bf16[1040,512]{1,0:T(8,128)(2,1)S(1)}, bf16[1040,512]{1,0:T(8,128)(2,1)S(1)}, u32[]{:S(2)}, u32[]{:S(2)}) collective-permute-start(bf16[1040,512]{1,0:T(8,128)(2,1)S(1)} %get-tuple-element.83.refs_0_.refs_4_.refs_5_), channel_id=1, source_target_pairs={{0,96},{16,112},{32,0},{48,16},{64,32},{80,48},{96,64},{112,80},{1... | collective-permute-start | bytes 3194888 | tf_op jit(solution)/shard_map/ppermute | solution.py:42
  12.3 3.8 %collective-permute-start.7 = (bf16[8,640,128]{2,1,0:T(8,128)(2,1)}, bf16[8,640,128]{2,1,0:T(8,128)(2,1)S(1)}, u32[]{:S(2)}, u32[]{:S(2)}) collective-permute-start(bf16[8,640,128]{2,1,0:T(8,128)(2,1)} %get-tuple-element.122.refs_0_), channel_id=1, source_target_pairs={{0,12},{1,13},{2,14},{3,15},{4,0},{5,1},{6,2},{7,3},{8,4},{9,5},{1... | collective-permute-start | bytes 3932168 | tf_op jit(solution)/shard_map/ppermute | solution.py:37
  16.0 18.4 %collective-permute-done.refs_1_.refs_6_.refs_7_ = bf16[1040,512]{1,0:T(8,128)(2,1)S(1)} collective-permute-done((bf16[1040,512]{1,0:T(8,128)(2,1)S(1)}, bf16[1040,512]{1,0:T(8,128)(2,1)S(1)}, u32[]{:S(2)}, u32[]{:S(2)}) %collective-permute-start) | collective-permute-done | bytes 1064992 | tf_op jit(solution)/shard_map/ppermute | solution.py:42
  36.0 6.4 %collective-permute-done.2.refs_3_.refs_10_.refs_11_ = bf16[1040,512]{1,0:T(8,128)(2,1)S(1)} collective-permute-done((bf16[1040,512]{1,0:T(8,128)(2,1)S(1)}, bf16[1040,512]{1,0:T(8,128)(2,1)S(1)}, u32[]{:S(2)}, u32[]{:S(2)}) %collective-permute-start.2) | collective-permute-done | bytes 1064992 | tf_op jit(solution)/shard_map/ppermute | solution.py:42
  46.2 9.4 %collective-permute-done.1.refs_2_.refs_9_ = bf16[528,512]{1,0:T(8,128)(2,1)} collective-permute-done((bf16[528,512]{1,0:T(8,128)(2,1)S(1)}, bf16[528,512]{1,0:T(8,128)(2,1)}, u32[]{:S(2)}, u32[]{:S(2)}) %collective-permute-start.1) | collective-permute-done | bytes 540704 | tf_op jit(solution)/shard_map/ppermute | solution.py:42
  71.9 10.5 %transform.4 = (bf16[4,2,128,128]{3,2,1,0:T(8,128)(2,1)S(1)}, bf16[4,2,128,128]{3,2,1,0:T(8,128)(2,1)S(1)}, bf16[4,2,128,128]{3,2,1,0:T(8,128)(2,1)S(1)}, bf16[4...) custom-call(s32[8,128]{1,0:T(8,128)S(1)} %copy-done.17, ...), custom_call_target="tpu_custom_call" | custom-call | flops 6442450944 | bytes 16777216 | tf_op jit(solution)/shard_map/transform/pallas_call | solution.py:154
  85.2 2.4 collective-permute-start.31
  87.7 8.3 %collective-permute-done.12.refs_1_ = bf16[4,2,128,128]{3,2,1,0:T(8,128)(2,1)S(1)} collective-permute-done((bf16[4,2,128,128]{3,2,1,0:T(8,128)(2,1)S(1)}, bf16[4,2,128,128]{3,2,1,0:T(8,128)(2,1)S(1)}, u32[]{:S(2)}, u32[]{:S(2)}) %collective-permute-start.12) | collective-permute-done | bytes 262176 | tf_op jit(solution)/shard_map/ppermute | solution.py:42
  97.5 2.9 %collective-permute-start.15 = (bf16[4,2,128,128]{3,2,1,0:T(8,128)(2,1)S(1)}, bf16[4,2,128,128]{3,2,1,0:T(8,128)(2,1)S(1)}, u32[]{:S(2)}, u32[]{:S(2)}) collective-permute-start(bf16[4,2,128,128]{3,2,1,0:T(8,128)(2,1)S(1)} %get-tuple-element.99), channel_id=1, source_target_pairs={{0,16},{16,0},{32,48},{48,32},{64,80},{80,64},{96,112},{112,96},{1... | collective-permute-start | bytes 786440 | tf_op jit(solution)/shard_map/ppermute | solution.py:42
  101.6 9.8 %collective-permute-done.16.refs_5_ = bf16[4,2,128,128]{3,2,1,0:T(8,128)(2,1)S(1)} collective-permute-done((bf16[4,2,128,128]{3,2,1,0:T(8,128)(2,1)S(1)}, bf16[4,2,128,128]{3,2,1,0:T(8,128)(2,1)S(1)}, u32[]{:S(2)}, u32[]{:S(2)}) %collective-permute-start.16) | collective-permute-done | bytes 262176 | tf_op jit(solution)/shard_map/ppermute | solution.py:42
  112.0 3.7 %collective-permute-done.31.refs_1_ = bf16[8,640,128]{2,1,0:T(8,128)(2,1)S(1)} collective-permute-done((bf16[8,640,128]{2,1,0:T(8,128)(2,1)}, bf16[8,640,128]{2,1,0:T(8,128)(2,1)S(1)}, u32[]{:S(2)}, u32[]{:S(2)}) %collective-permute-start.31) | collective-permute-done | bytes 1310752 | tf_op jit(solution)/shard_map/ppermute | solution.py:37
  115.7 3.5 %collective-permute-done.20.refs_1_ = bf16[8,640,128]{2,1,0:T(8,128)(2,1)S(1)} collective-permute-done((bf16[8,640,128]{2,1,0:T(8,128)(2,1)}, bf16[8,640,128]{2,1,0:T(8,128)(2,1)S(1)}, u32[]{:S(2)}, u32[]{:S(2)}) %collective-permute-start.20) | collective-permute-done | bytes 1310752 | tf_op jit(solution)/shard_map/ppermute | solution.py:37
  119.2 3.9 %collective-permute-start.17 = (bf16[4,2,128,128]{3,2,1,0:T(8,128)(2,1)S(1)}, bf16[4,2,128,128]{3,2,1,0:T(8,128)(2,1)S(1)}, u32[]{:S(2)}, u32[]{:S(2)}) collective-permute-start(bf16[4,2,128,128]{3,2,1,0:T(8,128)(2,1)S(1)} %get-tuple-element.101), channel_id=1, source_target_pairs={{0,80},{16,64},{32,112},{48,96},{64,16},{80,0},{96,48},{112,32},{1... | collective-permute-start | bytes 786440 | tf_op jit(solution)/shard_map/ppermute | solution.py:42
  123.1 10.8 %collective-permute-done.22.refs_3_ = bf16[8,640,128]{2,1,0:T(8,128)(2,1)S(1)} collective-permute-done((bf16[8,640,128]{2,1,0:T(8,128)(2,1)S(1)}, bf16[8,640,128]{2,1,0:T(8,128)(2,1)S(1)}, u32[]{:S(2)}, u32[]{:S(2)}) %collective-permute-start.22) | collective-permute-done | bytes 1310752 | tf_op jit(solution)/shard_map/ppermute | solution.py:37
  134.0 9.4 %transform.5 = (bf16[4,2,128,128]{3,2,1,0:T(8,128)(2,1)S(1)}, bf16[4,2,128,128]{3,2,1,0:T(8,128)(2,1)S(1)}, bf16[4,2,128,128]{3,2,1,0:T(8,128)(2,1)S(1)}, bf16[4...) custom-call(s32[8,128]{1,0:T(8,128)S(1)} %copy-done.18, ...), custom_call_target="tpu_custom_call" | custom-call | flops 6442450944 | bytes 16777216 | tf_op jit(solution)/shard_map/transform/pallas_call | solution.py:154
  147.8 9.7 %collective-permute-done.23.refs_1_ = bf16[4,2,128,128]{3,2,1,0:T(8,128)(2,1)S(1)} collective-permute-done((bf16[4,2,128,128]{3,2,1,0:T(8,128)(2,1)S(1)}, bf16[4,2,128,128]{3,2,1,0:T(8,128)(2,1)S(1)}, u32[]{:S(2)}, u32[]{:S(2)}) %collective-permute-start.23) | collective-permute-done | bytes 262176 | tf_op jit(solution)/shard_map/ppermute | solution.py:42
  158.5 2.5 collective-permute-start.28
  161.0 12.1 %collective-permute-done.27.refs_5_ = bf16[4,2,128,128]{3,2,1,0:T(8,128)(2,1)S(1)} collective-permute-done((bf16[4,2,128,128]{3,2,1,0:T(8,128)(2,1)S(1)}, bf16[4,2,128,128]{3,2,1,0:T(8,128)(2,1)S(1)}, u32[]{:S(2)}, u32[]{:S(2)}) %collective-permute-start.27) | collective-permute-done | bytes 262176 | tf_op jit(solution)/shard_map/ppermute | solution.py:42
  174.9 4.2 %cycle.4.refs_8_ = f32[8,128,128]{2,1,0:T(8,128)S(1)} custom-call(s32[256]{0:T(256)S(1)} %bitcast.10, s32[2]{0:T(128)S(1)} %pad_add_fusion.me, bf16[256,128,128]{2,1,0:T(8,128)(2,1)S(1)} %bitcast.6, bf16[4,2,128,128]{3,2,1,0:T(8,128)(2,1)S(1)} %get-tuple-element.95.refs_0_, bf16[4,2,128,128]{3,2,1,0:T(8,128)(2,1)S(1)} %collective-permute-done.12.refs_1_, ...), custom_call_target="tpu_custom_call" | custom-call | flops 2147483648 | bytes 6291456 | tf_op jit(solution)/shard_map/cycle/pallas_call | solution.py:212
  179.9 8.4 %transform.6 = (bf16[4,2,128,128]{3,2,1,0:T(8,128)(2,1)S(1)}, bf16[4,2,128,128]{3,2,1,0:T(8,128)(2,1)S(1)}, bf16[4,2,128,128]{3,2,1,0:T(8,128)(2,1)S(1)}, bf16[4...) custom-call(s32[8,128]{1,0:T(8,128)S(1)} %copy-done.18, ...), custom_call_target="tpu_custom_call" | custom-call | flops 6442450944 | bytes 16777216 | tf_op jit(solution)/shard_map/transform/pallas_call | solution.py:154
  188.3 4.2 %cycle.5.refs_8_ = f32[8,128,128]{2,1,0:T(8,128)S(1)} custom-call(s32[256]{0:T(256)S(1)} %bitcast.11, s32[2]{0:T(128)S(1)} %pad_add_fusion.me, bf16[256,128,128]{2,1,0:T(8,128)(2,1)S(1)} %bitcast.7, bf16[4,2,128,128]{3,2,1,0:T(8,128)(2,1)S(1)} %get-tuple-element.114.refs_0_, bf16[4,2,128,128]{3,2,1,0:T(8,128)(2,1)S(1)} %collective-permute-done.23.refs_1_, ...), custom_call_target="tpu_custom_call" | custom-call | flops 2147483648 | bytes 6291456 | tf_op jit(solution)/shard_map/cycle/pallas_call | solution.py:212
  198.1 9.2 %collective-permute-done.37.refs_3_ = bf16[8,640,128]{2,1,0:T(8,128)(2,1)S(1)} collective-permute-done((bf16[8,640,128]{2,1,0:T(8,128)(2,1)S(1)}, bf16[8,640,128]{2,1,0:T(8,128)(2,1)S(1)}, u32[]{:S(2)}, u32[]{:S(2)}) %collective-permute-start.37) | collective-permute-done | bytes 1310752 | tf_op jit(solution)/shard_map/ppermute | solution.py:37
  207.3 8.4 %transform.7 = (bf16[4,2,128,128]{3,2,1,0:T(8,128)(2,1)S(1)}, bf16[4,2,128,128]{3,2,1,0:T(8,128)(2,1)S(1)}, bf16[4,2,128,128]{3,2,1,0:T(8,128)(2,1)S(1)}, bf16[4...) custom-call(s32[8,128]{1,0:T(8,128)S(1)} %copy-done.18, ...), custom_call_target="tpu_custom_call" | custom-call | flops 6442450944 | bytes 16777216 | tf_op jit(solution)/shard_map/transform/pallas_call | solution.py:154
  222.3 3.3 %collective-permute-done.49.refs_5_ = bf16[4,2,128,128]{3,2,1,0:T(8,128)(2,1)S(1)} collective-permute-done((bf16[4,2,128,128]{3,2,1,0:T(8,128)(2,1)S(1)}, bf16[4,2,128,128]{3,2,1,0:T(8,128)(2,1)S(1)}, u32[]{:S(2)}, u32[]{:S(2)}) %collective-permute-start.49) | collective-permute-done | bytes 262176 | tf_op jit(solution)/shard_map/ppermute | solution.py:42
  226.3 5.4 %collective-permute-done.50.refs_6_ = bf16[4,2,128,128]{3,2,1,0:T(8,128)(2,1)S(1)} collective-permute-done((bf16[4,2,128,128]{3,2,1,0:T(8,128)(2,1)S(1)}, bf16[4,2,128,128]{3,2,1,0:T(8,128)(2,1)S(1)}, u32[]{:S(2)}, u32[]{:S(2)}) %collective-permute-start.50) | collective-permute-done | bytes 262176 | tf_op jit(solution)/shard_map/ppermute | solution.py:42
  233.4 3.5 %collective-permute-done.38.refs_1_ = bf16[4,2,128,128]{3,2,1,0:T(8,128)(2,1)S(1)} collective-permute-done((bf16[4,2,128,128]{3,2,1,0:T(8,128)(2,1)S(1)}, bf16[4,2,128,128]{3,2,1,0:T(8,128)(2,1)S(1)}, u32[]{:S(2)}, u32[]{:S(2)}) %collective-permute-start.38) | collective-permute-done | bytes 262176 | tf_op jit(solution)/shard_map/ppermute | solution.py:42
  237.3 6.1 %collective-permute-done.39.refs_2_ = bf16[4,2,128,128]{3,2,1,0:T(8,128)(2,1)S(1)} collective-permute-done((bf16[4,2,128,128]{3,2,1,0:T(8,128)(2,1)S(1)}, bf16[4,2,128,128]{3,2,1,0:T(8,128)(2,1)S(1)}, u32[]{:S(2)}, u32[]{:S(2)}) %collective-permute-start.39) | collective-permute-done | bytes 262176 | tf_op jit(solution)/shard_map/ppermute | solution.py:42
  243.4 4.2 %cycle.6.refs_8_ = f32[8,128,128]{2,1,0:T(8,128)S(1)} custom-call(s32[256]{0:T(256)S(1)} %bitcast.12, s32[2]{0:T(128)S(1)} %pad_add_fusion.me, bf16[256,128,128]{2,1,0:T(8,128)(2,1)S(1)} %bitcast.8, bf16[4,2,128,128]{3,2,1,0:T(8,128)(2,1)S(1)} %get-tuple-element.151.refs_0_, bf16[4,2,128,128]{3,2,1,0:T(8,128)(2,1)S(1)} %collective-permute-done.45.refs_1_, ...), custom_call_target="tpu_custom_call" | custom-call | flops 2147483648 | bytes 6291456 | tf_op jit(solution)/shard_map/cycle/pallas_call | solution.py:212
  248.1 6.1 %collective-permute-done.43.refs_6_ = bf16[4,2,128,128]{3,2,1,0:T(8,128)(2,1)S(1)} collective-permute-done((bf16[4,2,128,128]{3,2,1,0:T(8,128)(2,1)S(1)}, bf16[4,2,128,128]{3,2,1,0:T(8,128)(2,1)S(1)}, u32[]{:S(2)}, u32[]{:S(2)}) %collective-permute-start.43) | collective-permute-done | bytes 262176 | tf_op jit(solution)/shard_map/ppermute | solution.py:42
  254.5 4.2 %cycle.7.own = bf16[8,128,128]{2,1,0:T(8,128)(2,1)S(1)} custom-call(s32[256]{0:T(256)S(1)} %bitcast.13, s32[2]{0:T(128)S(1)} %pad_add_fusion.me, bf16[256,128,128]{2,1,0:T(8,128)(2,1)S(1)} %bitcast.9, bf16[4,2,128,128]{3,2,1,0:T(8,128)(2,1)S(1)} %get-tuple-element.143.refs_0_, bf16[4,2,128,128]{3,2,1,0:T(8,128)(2,1)S(1)} %collective-permute-done.38.refs_1_, ...), custom_call_target="tpu_custom_call" | custom-call | flops 2147483648 | bytes 6291456 | tf_op jit(solution)/shard_map/cycle/pallas_call | solution.py:212
  259.7 8.0 %collective-permute-done.52.partner = bf16[8,128,128]{2,1,0:T(8,128)(2,1)S(1)} collective-permute-done((bf16[8,128,128]{2,1,0:T(8,128)(2,1)S(1)}, bf16[8,128,128]{2,1,0:T(8,128)(2,1)S(1)}, u32[]{:S(2)}, u32[]{:S(2)}) %collective-permute-start.52) | collective-permute-done | bytes 262176 | tf_op jit(solution)/shard_map/ppermute | solution.py:454
  (146 shorter events, 57.5 us)
Async XLA Ops:
  8.7 25.7 %collective-permute-start = (bf16[1040,512]{1,0:T(8,128)(2,1)S(1)}, bf16[1040,512]{1,0:T(8,128)(2,1)S(1)}, u32[]{:S(2)}, u32[]{:S(2)}) collective-permute-start(bf16[1040,512]{1,0:T(8,128)(2,1)S(1)} %get-tuple-element.83.refs_0_.refs_4_.refs_5_), channel_id=1, source_target_pairs={{0,96},{16,112},{32,0},{48,16},{64,32},{80,48},{96,64},{112,80},{1... | collective-permute-start | bytes 3194888 | tf_op jit(solution)/shard_map/ppermute | solution.py:42
  12.3 30.2 %collective-permute-start.7 = (bf16[8,640,128]{2,1,0:T(8,128)(2,1)}, bf16[8,640,128]{2,1,0:T(8,128)(2,1)S(1)}, u32[]{:S(2)}, u32[]{:S(2)}) collective-permute-start(bf16[8,640,128]{2,1,0:T(8,128)(2,1)} %get-tuple-element.122.refs_0_), channel_id=1, source_target_pairs={{0,12},{1,13},{2,14},{3,15},{4,0},{5,1},{6,2},{7,3},{8,4},{9,5},{1... | collective-permute-start | bytes 3932168 | tf_op jit(solution)/shard_map/ppermute | solution.py:37
  16.0 26.3 %collective-permute-start.2 = (bf16[1040,512]{1,0:T(8,128)(2,1)S(1)}, bf16[1040,512]{1,0:T(8,128)(2,1)S(1)}, u32[]{:S(2)}, u32[]{:S(2)}) collective-permute-start(bf16[1040,512]{1,0:T(8,128)(2,1)S(1)} %get-tuple-element.83.refs_0_.refs_4_.refs_5_), channel_id=1, source_target_pairs={{0,32},{16,48},{32,64},{48,80},{64,96},{80,112},{96,0},{112,16},{1... | collective-permute-start | bytes 3194888 | tf_op jit(solution)/shard_map/ppermute | solution.py:42
  16.0 28.5 %collective-permute-start.8 = (bf16[8,640,128]{2,1,0:T(8,128)(2,1)}, bf16[8,640,128]{2,1,0:T(8,128)(2,1)}, u32[]{:S(2)}, u32[]{:S(2)}) collective-permute-start(bf16[8,640,128]{2,1,0:T(8,128)(2,1)} %get-tuple-element.122.refs_0_), channel_id=1, source_target_pairs={{0,4},{1,5},{2,6},{3,7},{4,8},{5,9},{6,10},{7,11},{8,12},{9,13},{1... | collective-permute-start | bytes 3932168 | tf_op jit(solution)/shard_map/ppermute | solution.py:37
  16.0 26.4 %collective-permute-start.3 = (bf16[1040,512]{1,0:T(8,128)(2,1)S(1)}, bf16[1040,512]{1,0:T(8,128)(2,1)S(1)}, u32[]{:S(2)}, u32[]{:S(2)}) collective-permute-start(bf16[1040,512]{1,0:T(8,128)(2,1)S(1)} %get-tuple-element.83.refs_0_.refs_4_.refs_5_), channel_id=1, source_target_pairs={{0,16},{16,0},{32,48},{48,32},{64,80},{80,64},{96,112},{112,96},{1... | collective-permute-start | bytes 3194888 | tf_op jit(solution)/shard_map/ppermute | solution.py:42
  34.5 25.8 %collective-permute-start.4 = (bf16[1040,512]{1,0:T(8,128)(2,1)S(1)}, bf16[1040,512]{1,0:T(8,128)(2,1)S(1)}, u32[]{:S(2)}, u32[]{:S(2)}) collective-permute-start(bf16[1040,512]{1,0:T(8,128)(2,1)S(1)} %collective-permute-done.refs_1_.refs_6_.refs_7_), channel_id=1, source_target_pairs={{0,16},{16,0},{32,48},{48,32},{64,80},{80,64},{96,112},{112,96},{1... | collective-permute-start | bytes 3194888 | tf_op jit(solution)/shard_map/ppermute | solution.py:42
  42.3 21.4 %collective-permute-start.9 = (bf16[8,640,128]{2,1,0:T(8,128)(2,1)}, bf16[8,640,128]{2,1,0:T(8,128)(2,1)}, u32[]{:S(2)}, u32[]{:S(2)}) collective-permute-start(bf16[8,640,128]{2,1,0:T(8,128)(2,1)} %get-tuple-element.122.refs_0_), channel_id=1, source_target_pairs={{0,1},{1,2},{2,3},{3,0},{4,5},{5,6},{6,7},{7,4},{8,9},{9,10},{10,1... | collective-permute-start | bytes 3932168 | tf_op jit(solution)/shard_map/ppermute | solution.py:37
  43.7 18.5 %collective-permute-start.6 = (bf16[1040,512]{1,0:T(8,128)(2,1)S(1)}, bf16[1040,512]{1,0:T(8,128)(2,1)}, u32[]{:S(2)}, u32[]{:S(2)}) collective-permute-start(bf16[1040,512]{1,0:T(8,128)(2,1)S(1)} %collective-permute-done.2.refs_3_.refs_10_.refs_11_), channel_id=1, source_target_pairs={{0,16},{16,0},{32,48},{48,32},{64,80},{80,64},{96,112},{112,96},{1... | collective-permute-start | bytes 3194888 | tf_op jit(solution)/shard_map/ppermute | solution.py:42
  60.3 27.4 %collective-permute-start.19 = (bf16[8,640,128]{2,1,0:T(8,128)(2,1)}, bf16[8,640,128]{2,1,0:T(8,128)(2,1)}, u32[]{:S(2)}, u32[]{:S(2)}) collective-permute-start(bf16[8,640,128]{2,1,0:T(8,128)(2,1)} %get-tuple-element.122.refs_0_), channel_id=1, source_target_pairs={{0,3},{1,0},{2,1},{3,2},{4,7},{5,4},{6,5},{7,6},{8,11},{9,8},{10,9... | collective-permute-start | bytes 3932168 | tf_op jit(solution)/shard_map/ppermute | solution.py:37
  85.2 30.4 %collective-permute-start.31 = (bf16[8,640,128]{2,1,0:T(8,128)(2,1)}, bf16[8,640,128]{2,1,0:T(8,128)(2,1)S(1)}, u32[]{:S(2)}, u32[]{:S(2)}) collective-permute-start(bf16[8,640,128]{2,1,0:T(8,128)(2,1)} %get-tuple-element.122.refs_0_), channel_id=1, source_target_pairs={{0,8},{1,9},{2,10},{3,11},{4,12},{5,13},{6,14},{7,15},{8,0},{9,1},... | collective-permute-start | bytes 3932168 | tf_op jit(solution)/shard_map/ppermute | solution.py:37
  87.7 31.5 %collective-permute-start.20 = (bf16[8,640,128]{2,1,0:T(8,128)(2,1)}, bf16[8,640,128]{2,1,0:T(8,128)(2,1)S(1)}, u32[]{:S(2)}, u32[]{:S(2)}) collective-permute-start(bf16[8,640,128]{2,1,0:T(8,128)(2,1)} %collective-permute-done.8.refs_2_), channel_id=1, source_target_pairs={{0,1},{1,2},{2,3},{3,0},{4,5},{5,6},{6,7},{7,4},{8,9},{9,10},{10,1... | collective-permute-start | bytes 3932168 | tf_op jit(solution)/shard_map/ppermute | solution.py:37
  96.0 27.1 %collective-permute-start.21 = (bf16[8,640,128]{2,1,0:T(8,128)(2,1)S(1)}, bf16[8,640,128]{2,1,0:T(8,128)(2,1)S(1)}, u32[]{:S(2)}, u32[]{:S(2)}) collective-permute-start(bf16[8,640,128]{2,1,0:T(8,128)(2,1)S(1)} %copy-done.22), channel_id=1, source_target_pairs={{0,3},{1,0},{2,1},{3,2},{4,7},{5,4},{6,5},{7,6},{8,11},{9,8},{10,9... | collective-permute-start | bytes 3932168 | tf_op jit(solution)/shard_map/ppermute | solution.py:37
  97.5 36.4 %collective-permute-start.22 = (bf16[8,640,128]{2,1,0:T(8,128)(2,1)S(1)}, bf16[8,640,128]{2,1,0:T(8,128)(2,1)S(1)}, u32[]{:S(2)}, u32[]{:S(2)}) collective-permute-start(bf16[8,640,128]{2,1,0:T(8,128)(2,1)S(1)} %copy-done.22), channel_id=1, source_target_pairs={{0,1},{1,2},{2,3},{3,0},{4,5},{5,6},{6,7},{7,4},{8,9},{9,10},{10,1... | collective-permute-start | bytes 3932168 | tf_op jit(solution)/shard_map/ppermute | solution.py:37
  111.4 34.4 %collective-permute-start.30 = (bf16[8,640,128]{2,1,0:T(8,128)(2,1)}, bf16[8,640,128]{2,1,0:T(8,128)(2,1)S(1)}, u32[]{:S(2)}, u32[]{:S(2)}) collective-permute-start(bf16[8,640,128]{2,1,0:T(8,128)(2,1)} %collective-permute-done.8.refs_2_), channel_id=1, source_target_pairs={{0,3},{1,0},{2,1},{3,2},{4,7},{5,4},{6,5},{7,6},{8,11},{9,8},{10,9... | collective-permute-start | bytes 3932168 | tf_op jit(solution)/shard_map/ppermute | solution.py:37
  115.7 59.1 %collective-permute-start.32 = (bf16[8,640,128]{2,1,0:T(8,128)(2,1)S(1)}, bf16[8,640,128]{2,1,0:T(8,128)(2,1)S(1)}, u32[]{:S(2)}, u32[]{:S(2)}) collective-permute-start(bf16[8,640,128]{2,1,0:T(8,128)(2,1)S(1)} %collective-permute-done.31.refs_1_), channel_id=1, source_target_pairs={{0,1},{1,2},{2,3},{3,0},{4,5},{5,6},{6,7},{7,4},{8,9},{9,10},{10,1... | collective-permute-start | bytes 3932168 | tf_op jit(solution)/shard_map/ppermute | solution.py:37
  119.2 24.2 %collective-permute-start.17 = (bf16[4,2,128,128]{3,2,1,0:T(8,128)(2,1)S(1)}, bf16[4,2,128,128]{3,2,1,0:T(8,128)(2,1)S(1)}, u32[]{:S(2)}, u32[]{:S(2)}) collective-permute-start(bf16[4,2,128,128]{3,2,1,0:T(8,128)(2,1)S(1)} %get-tuple-element.101), channel_id=1, source_target_pairs={{0,80},{16,64},{32,112},{48,96},{64,16},{80,0},{96,48},{112,32},{1... | collective-permute-start | bytes 786440 | tf_op jit(solution)/shard_map/ppermute | solution.py:42
  123.1 20.9 %collective-permute-start.18 = (bf16[4,2,128,128]{3,2,1,0:T(8,128)(2,1)S(1)}, bf16[4,2,128,128]{3,2,1,0:T(8,128)(2,1)S(1)}, u32[]{:S(2)}, u32[]{:S(2)}) collective-permute-start(bf16[4,2,128,128]{3,2,1,0:T(8,128)(2,1)S(1)} %get-tuple-element.102), channel_id=1, source_target_pairs={{0,112},{16,96},{32,16},{48,0},{64,48},{80,32},{96,80},{112,64},{1... | collective-permute-start | bytes 786440 | tf_op jit(solution)/shard_map/ppermute | solution.py:42
  133.9 45.3 %collective-permute-start.33 = (bf16[8,640,128]{2,1,0:T(8,128)(2,1)S(1)}, bf16[8,640,128]{2,1,0:T(8,128)(2,1)S(1)}, u32[]{:S(2)}, u32[]{:S(2)}) collective-permute-start(bf16[8,640,128]{2,1,0:T(8,128)(2,1)S(1)} %collective-permute-done.31.refs_1_), channel_id=1, source_target_pairs={{0,3},{1,0},{2,1},{3,2},{4,7},{5,4},{6,5},{7,6},{8,11},{9,8},{10,9... | collective-permute-start | bytes 3932168 | tf_op jit(solution)/shard_map/ppermute | solution.py:37
  158.5 15.8 %collective-permute-start.28 = (bf16[4,2,128,128]{3,2,1,0:T(8,128)(2,1)S(1)}, bf16[4,2,128,128]{3,2,1,0:T(8,128)(2,1)S(1)}, u32[]{:S(2)}, u32[]{:S(2)}) collective-permute-start(bf16[4,2,128,128]{3,2,1,0:T(8,128)(2,1)S(1)} %get-tuple-element.120), channel_id=1, source_target_pairs={{0,80},{16,64},{32,112},{48,96},{64,16},{80,0},{96,48},{112,32},{1... | collective-permute-start | bytes 786440 | tf_op jit(solution)/shard_map/ppermute | solution.py:42
  161.0 33.1 %collective-permute-start.34 = (bf16[8,640,128]{2,1,0:T(8,128)(2,1)}, bf16[8,640,128]{2,1,0:T(8,128)(2,1)S(1)}, u32[]{:S(2)}, u32[]{:S(2)}) collective-permute-start(bf16[8,640,128]{2,1,0:T(8,128)(2,1)} %collective-permute-done.9.refs_3_), channel_id=1, source_target_pairs={{0,1},{1,2},{2,3},{3,0},{4,5},{5,6},{6,7},{7,4},{8,9},{9,10},{10,1... | collective-permute-start | bytes 3932168 | tf_op jit(solution)/shard_map/ppermute | solution.py:37
  173.1 21.8 %collective-permute-start.35 = (bf16[8,640,128]{2,1,0:T(8,128)(2,1)S(1)}, bf16[8,640,128]{2,1,0:T(8,128)(2,1)S(1)}, u32[]{:S(2)}, u32[]{:S(2)}) collective-permute-start(bf16[8,640,128]{2,1,0:T(8,128)(2,1)S(1)} %collective-permute-done.21.refs_2_), channel_id=1, source_target_pairs={{0,3},{1,0},{2,1},{3,2},{4,7},{5,4},{6,5},{7,6},{8,11},{9,8},{10,9... | collective-permute-start | bytes 3932168 | tf_op jit(solution)/shard_map/ppermute | solution.py:37
  174.3 22.3 %collective-permute-start.36 = (bf16[8,640,128]{2,1,0:T(8,128)(2,1)S(1)}, bf16[8,640,128]{2,1,0:T(8,128)(2,1)S(1)}, u32[]{:S(2)}, u32[]{:S(2)}) collective-permute-start(bf16[8,640,128]{2,1,0:T(8,128)(2,1)S(1)} %collective-permute-done.31.refs_1_), channel_id=1, source_target_pairs={{0,2},{1,3},{2,0},{3,1},{4,6},{5,7},{6,4},{7,5},{8,10},{9,11},{10,... | collective-permute-start | bytes 3932168 | tf_op jit(solution)/shard_map/ppermute | solution.py:37
  174.8 32.5 %collective-permute-start.37 = (bf16[8,640,128]{2,1,0:T(8,128)(2,1)S(1)}, bf16[8,640,128]{2,1,0:T(8,128)(2,1)S(1)}, u32[]{:S(2)}, u32[]{:S(2)}) collective-permute-start(bf16[8,640,128]{2,1,0:T(8,128)(2,1)S(1)} %collective-permute-done.20.refs_1_), channel_id=1, source_target_pairs={{0,1},{1,2},{2,3},{3,0},{4,5},{5,6},{6,7},{7,4},{8,9},{9,10},{10,1... | collective-permute-start | bytes 3932168 | tf_op jit(solution)/shard_map/ppermute | solution.py:37
  192.5 25.0 %collective-permute-start.45 = (bf16[4,2,128,128]{3,2,1,0:T(8,128)(2,1)S(1)}, bf16[4,2,128,128]{3,2,1,0:T(8,128)(2,1)S(1)}, u32[]{:S(2)}, u32[]{:S(2)}) collective-permute-start(bf16[4,2,128,128]{3,2,1,0:T(8,128)(2,1)S(1)} %get-tuple-element.152), channel_id=1, source_target_pairs={{0,32},{16,48},{32,64},{48,80},{64,96},{80,112},{96,0},{112,16},{1... | collective-permute-start | bytes 786440 | tf_op jit(solution)/shard_map/ppermute | solution.py:42
  194.1 25.2 %collective-permute-start.46 = (bf16[4,2,128,128]{3,2,1,0:T(8,128)(2,1)S(1)}, bf16[4,2,128,128]{3,2,1,0:T(8,128)(2,1)S(1)}, u32[]{:S(2)}, u32[]{:S(2)}) collective-permute-start(bf16[4,2,128,128]{3,2,1,0:T(8,128)(2,1)S(1)} %get-tuple-element.153), channel_id=1, source_target_pairs={{0,64},{16,80},{32,96},{48,112},{64,0},{80,16},{96,32},{112,48},{1... | collective-permute-start | bytes 786440 | tf_op jit(solution)/shard_map/ppermute | solution.py:42
  194.9 24.8 %collective-permute-start.47 = (bf16[4,2,128,128]{3,2,1,0:T(8,128)(2,1)S(1)}, bf16[4,2,128,128]{3,2,1,0:T(8,128)(2,1)S(1)}, u32[]{:S(2)}, u32[]{:S(2)}) collective-permute-start(bf16[4,2,128,128]{3,2,1,0:T(8,128)(2,1)S(1)} %get-tuple-element.154), channel_id=1, source_target_pairs={{0,96},{16,112},{32,0},{48,16},{64,32},{80,48},{96,64},{112,80},{1... | collective-permute-start | bytes 786440 | tf_op jit(solution)/shard_map/ppermute | solution.py:42
  196.6 25.1 %collective-permute-start.48 = (bf16[4,2,128,128]{3,2,1,0:T(8,128)(2,1)S(1)}, bf16[4,2,128,128]{3,2,1,0:T(8,128)(2,1)S(1)}, u32[]{:S(2)}, u32[]{:S(2)}) collective-permute-start(bf16[4,2,128,128]{3,2,1,0:T(8,128)(2,1)S(1)} %get-tuple-element.155), channel_id=1, source_target_pairs={{0,16},{16,0},{32,48},{48,32},{64,80},{80,64},{96,112},{112,96},{1... | collective-permute-start | bytes 786440 | tf_op jit(solution)/shard_map/ppermute | solution.py:42
  219.7 17.2 %collective-permute-start.38 = (bf16[4,2,128,128]{3,2,1,0:T(8,128)(2,1)S(1)}, bf16[4,2,128,128]{3,2,1,0:T(8,128)(2,1)S(1)}, u32[]{:S(2)}, u32[]{:S(2)}) collective-permute-start(bf16[4,2,128,128]{3,2,1,0:T(8,128)(2,1)S(1)} %get-tuple-element.144), channel_id=1, source_target_pairs={{0,32},{16,48},{32,64},{48,80},{64,96},{80,112},{96,0},{112,16},{1... | collective-permute-start | bytes 786440 | tf_op jit(solution)/shard_map/ppermute | solution.py:42
  221.7 21.7 %collective-permute-start.39 = (bf16[4,2,128,128]{3,2,1,0:T(8,128)(2,1)S(1)}, bf16[4,2,128,128]{3,2,1,0:T(8,128)(2,1)S(1)}, u32[]{:S(2)}, u32[]{:S(2)}) collective-permute-start(bf16[4,2,128,128]{3,2,1,0:T(8,128)(2,1)S(1)} %get-tuple-element.145), channel_id=1, source_target_pairs={{0,64},{16,80},{32,96},{48,112},{64,0},{80,16},{96,32},{112,48},{1... | collective-permute-start | bytes 786440 | tf_op jit(solution)/shard_map/ppermute | solution.py:42
  225.6 22.1 %collective-permute-start.40 = (bf16[4,2,128,128]{3,2,1,0:T(8,128)(2,1)S(1)}, bf16[4,2,128,128]{3,2,1,0:T(8,128)(2,1)S(1)}, u32[]{:S(2)}, u32[]{:S(2)}) collective-permute-start(bf16[4,2,128,128]{3,2,1,0:T(8,128)(2,1)S(1)} %get-tuple-element.146), channel_id=1, source_target_pairs={{0,96},{16,112},{32,0},{48,16},{64,32},{80,48},{96,64},{112,80},{1... | collective-permute-start | bytes 786440 | tf_op jit(solution)/shard_map/ppermute | solution.py:42
  231.7 16.0 %collective-permute-start.41 = (bf16[4,2,128,128]{3,2,1,0:T(8,128)(2,1)S(1)}, bf16[4,2,128,128]{3,2,1,0:T(8,128)(2,1)S(1)}, u32[]{:S(2)}, u32[]{:S(2)}) collective-permute-start(bf16[4,2,128,128]{3,2,1,0:T(8,128)(2,1)S(1)} %get-tuple-element.147), channel_id=1, source_target_pairs={{0,16},{16,0},{32,48},{48,32},{64,80},{80,64},{96,112},{112,96},{1... | collective-permute-start | bytes 786440 | tf_op jit(solution)/shard_map/ppermute | solution.py:42
  236.8 17.3 %collective-permute-start.43 = (bf16[4,2,128,128]{3,2,1,0:T(8,128)(2,1)S(1)}, bf16[4,2,128,128]{3,2,1,0:T(8,128)(2,1)S(1)}, u32[]{:S(2)}, u32[]{:S(2)}) collective-permute-start(bf16[4,2,128,128]{3,2,1,0:T(8,128)(2,1)S(1)} %get-tuple-element.149), channel_id=1, source_target_pairs={{0,80},{16,64},{32,112},{48,96},{64,16},{80,0},{96,48},{112,32},{1... | collective-permute-start | bytes 786440 | tf_op jit(solution)/shard_map/ppermute | solution.py:42
  (48 other events, 971.1 us)
where the time goes:
time: 272 us; the launch traced here: 271 us
  waiting for transfers between devices  139 us (51%)
  Pallas kernels  63.2 us (23%)
  starting transfers between devices  54.6 us (20%)
  local copies, waits for them, and re-layouts  12.3 us (5%)
    ppermute x37, waiting for transfers between devices, shift_ia(): lax.ppermute(value, 'ia', [(i, (i // 2 + steps) % RING * 2 + (i % 2 ^ fli...  104 us
    ppermute x37, starting transfers between devices, shift_ia(): lax.ppermute(value, 'ia', [(i, (i // 2 + steps) % RING * 2 + (i % 2 ^ fli...  42.3 us
    pallas_call x4, Pallas kernels, transform(): pl.pallas_call(functools.partial(transform_kernel, chunk, tuple((start fo...  36.7 us
    ppermute x15, waiting for transfers between devices, shift_ja(): return lax.ppermute(value, AXES, ring_perm(stage, shift))  27.2 us
    pallas_call x4, Pallas kernels, cycle_part(): pl.pallas_call(functools.partial(cycle_kernel, chunk), out_shape=jax.Shap...  16.8 us
    ppermute x15, starting transfers between devices, shift_ja(): return lax.ppermute(value, AXES, ring_perm(stage, shift))  11.9 us
    unnamed x54, local copies, waits for them, and re-layouts  11.5 us
    ppermute x1, waiting for transfers between devices, update(): lax.ppermute(cycle_sum, 'ja', [(b, b ^ apart) for b in range(2 * apart)])  7.96 us
  transfers between devices with their start and end apart: 53, of which 23 were waited for; matrix products, arithmetic and copies ran while one was open for 0% of the time, Pallas kernels for 19%

commit v1 on v0

--- a/solution.py
+++ b/solution.py
@@ -12,9 +12,9 @@
 AXES = ("ia", "ja")
 CHUNKS = (
     ((0, 0), (0, 1), (0, 3), (3, 0)),
-    ((1, 0), (3, 3), (1, 1), (3, 1)),
-    ((1, 3), (0, 2), (3, 2), (1, 2)),
-    ((2, 0), (2, 1), (2, 2), (2, 3)),
+    ((1, 0), (3, 3), (1, 1), (0, 2)),
+    ((3, 1), (1, 3), (3, 2), (1, 2)),
+    ((2, 0), (2, 1), (2, 3), (2, 2)),
 )
 NOTES = 16
 NT = (((1,), (1,)), ((), ()))
@@ -334,6 +334,7 @@
             pltpu.VMEM((8, NOTES, devices), jnp.bfloat16),
             pltpu.SemaphoreType.DMA((8,)),
         ],
+        compiler_params=pltpu.CompilerParams(vmem_limit_bytes=2 << 20),
         name="notes",
     )(*lines)
 
@@ -365,6 +366,7 @@
         ),
         in_specs=[smem] * 3 + [vmem] * 5,
         out_specs=(vmem, vmem),
+        compiler_params=pltpu.CompilerParams(vmem_limit_bytes=12 << 20),
         name="finish",
     )(rev, count, occ, exchange, amps, own, partner, energy)
 
@@ -396,18 +398,17 @@
     first = {0: block}
     first[3] = shift_ja(block, 1, 1)
     first[1] = shift_ja(block, 1, -1)
+    block, first[1], first[3] = lax.optimization_barrier((block, first[1], first[3]))
     held = {}
-    held[3, 0] = shift_ja(block, 2, 1)
-    held[1, 0] = shift_ja(block, 2, -1)
-
+    for u, shift in ((3, 1), (1, -1)):
+        held[u, 0] = shift_ja(block, 2, shift)
+    first[2] = shift_ja(block, 1, 2)
     far_a = shift_ia(below[:half], 1, 0)
     far_b = shift_ia(above[half:], -1, 0)
-    block, first[1], first[3] = lax.optimization_barrier((block, first[1], first[3]))
-    for t in (3, 1):
-        held[3, t] = shift_ja(first[t], 2, 1)
-    for t in (1, 3):
-        held[1, t] = shift_ja(first[t], 2, -1)
-    first[2] = shift_ja(block, 1, 2)
+    for u, t, shift in ((3, 3, 1), (1, 1, -1)):
+        held[u, t] = shift_ja(first[t], 2, shift)
+    for u, t, shift in ((3, 1, 1), (1, 3, -1)):
+        held[u, t] = shift_ja(first[t], 2, shift)
     near = []
     for value in (line, above, below):
         near.append(shift_ia(value, 0, 1))
@@ -441,9 +442,8 @@
             held[0, 2] = first[2]
             for u, shift in ((3, 1), (1, -1)):
                 held[u, 2] = shift_ja(first[2], 2, shift)
-            for u, t, shift in ((3, 0, 1), (1, 1, -1), (3, 3, 1)):
+            for u, t, shift in ((3, 0, 1), (1, 1, -1), (3, 3, 1), (1, 2, -1)):
                 held[2, t] = shift_ja(held[u, t], 2, shift)
-            held[2, 2] = shift_ja(first[2], 2, 2)
         back = [sent[0]]
         for r in range(1, 8):
             back.append(shift_ia(sent[r], r & 3, r >> 2))

time: 272 us -> 248 us (0.912)
  the two profiles are of different devices: /device:TPU:1 before, /device:TPU:102 now
where the time goes in v1:
time: 248 us; the launch traced here: 245 us
  waiting for transfers between devices  104 us (42%)
  starting transfers between devices  62.5 us (25%)
  Pallas kernels  60.9 us (25%)
  local copies, waits for them, and re-layouts  17.3 us (7%)
    ppermute x37, waiting for transfers between devices, shift_ia(): lax.ppermute(value, 'ia', [(i, (i // 2 + steps) % RING * 2 + (i % 2 ^ fli...  73.5 us
    ppermute x37, starting transfers between devices, shift_ia(): lax.ppermute(value, 'ia', [(i, (i // 2 + steps) % RING * 2 + (i % 2 ^ fli...  40.6 us
    pallas_call x4, Pallas kernels, transform(): pl.pallas_call(functools.partial(transform_kernel, chunk, tuple((start fo...  36.3 us
    ppermute x15, starting transfers between devices, shift_ja(): return lax.ppermute(value, AXES, ring_perm(stage, shift))  21.8 us
    ppermute x15, waiting for transfers between devices, shift_ja(): return lax.ppermute(value, AXES, ring_perm(stage, shift))  19.8 us
    pallas_call x4, Pallas kernels, cycle_part(): pl.pallas_call(functools.partial(cycle_kernel, chunk), out_shape=jax.Shap...  16.8 us
    unnamed x62, local copies, waits for them, and re-layouts  16.4 us
    ppermute x1, waiting for transfers between devices, update(): lax.ppermute(cycle_sum, 'ja', [(b, b ^ apart) for b in range(2 * apart)])  10.5 us
  transfers between devices with their start and end apart: 53, of which 17 were waited for; matrix products, arithmetic and copies ran while one was open for 0% of the time, Pallas kernels for 20%

profile of v1, /device:TPU:102, one launch (start us, length us, event | category | flops | bytes accessed | tf_op | source)
XLA Modules:
  0.0 245.5 jit_solution(8536554029998538885)
XLA Ops:
  2.1 5.9 %prep.1 = (bf16[8,640,128]{2,1,0:T(8,128)(2,1)}, bf16[1040,512]{1,0:T(8,128)(2,1)S(1)}, bf16[8,128,128]{2,1,0:T(8,128)(2,1)S(1)}, s32[2,128]{1,0:T(2,128)S(1)}) custom-call(s32[8]{0:T(128)S(1)} %copy-done.17, s32[1,256]{1,0:T(1,128)S(1)} %reshape.13.entries, bf16[8,128,128]{2,1,0:T(8,128)(2,1)} %amps.1, bf16[8,512,128]{2,1,0:T(8,128)(2,1)} %bases.1), custom_call_target="tpu_custom_call" | custom-call | bytes 5242880 | tf_op jit(solution)/shard_map/prep/pallas_call | solution.py:281
  8.0 3.0 %collective-permute-start = (bf16[1040,512]{1,0:T(8,128)(2,1)S(1)}, bf16[1040,512]{1,0:T(8,128)(2,1)S(1)}, u32[]{:S(2)}, u32[]{:S(2)}) collective-permute-start(bf16[1040,512]{1,0:T(8,128)(2,1)S(1)} %get-tuple-element.83.refs_0_.refs_4_.refs_5_), channel_id=1, source_target_pairs={{0,96},{16,112},{32,0},{48,16},{64,32},{80,48},{96,64},{112,80},{1... | collective-permute-start | bytes 3194888 | tf_op jit(solution)/shard_map/ppermute | solution.py:42
  11.8 2.4 collective-permute-start.8
  14.2 19.5 %collective-permute-done.refs_1_.refs_6_.refs_7_ = bf16[1040,512]{1,0:T(8,128)(2,1)S(1)} collective-permute-done((bf16[1040,512]{1,0:T(8,128)(2,1)S(1)}, bf16[1040,512]{1,0:T(8,128)(2,1)S(1)}, u32[]{:S(2)}, u32[]{:S(2)}) %collective-permute-start) | collective-permute-done | bytes 1064992 | tf_op jit(solution)/shard_map/ppermute | solution.py:42
  33.8 3.8 %collective-permute-start.1 = (bf16[528,512]{1,0:T(8,128)(2,1)S(1)}, bf16[528,512]{1,0:T(8,128)(2,1)S(1)}, u32[]{:S(2)}, u32[]{:S(2)}) collective-permute-start(bf16[528,512]{1,0:T(8,128)(2,1)S(1)} %slice.8), channel_id=1, source_target_pairs={{0,96},{16,112},{32,0},{48,16},{64,32},{80,48},{96,64},{112,80},{1... | collective-permute-start | bytes 1622024 | tf_op jit(solution)/shard_map/ppermute | solution.py:42
  40.2 11.2 %collective-permute-done.10.refs_8_ = bf16[512,512]{1,0:T(8,128)(2,1)S(1)} collective-permute-done((bf16[512,512]{1,0:T(8,128)(2,1)S(1)}, bf16[512,512]{1,0:T(8,128)(2,1)S(1)}, u32[]{:S(2)}, u32[]{:S(2)}) %collective-permute-start.10) | collective-permute-done | bytes 524320 | tf_op jit(solution)/shard_map/ppermute | solution.py:42
  61.9 2.8 %collective-permute-start.30 = (bf16[8,640,128]{2,1,0:T(8,128)(2,1)}, bf16[8,640,128]{2,1,0:T(8,128)(2,1)}, u32[]{:S(2)}, u32[]{:S(2)}) collective-permute-start(bf16[8,640,128]{2,1,0:T(8,128)(2,1)} %collective-permute-done.7.refs_1_), channel_id=1, source_target_pairs={{0,1},{1,2},{2,3},{3,0},{4,5},{5,6},{6,7},{7,4},{8,9},{9,10},{10,1... | collective-permute-start | bytes 3932168 | tf_op jit(solution)/shard_map/ppermute | solution.py:37
  67.1 3.5 %collective-permute-start.31 = (bf16[8,640,128]{2,1,0:T(8,128)(2,1)}, bf16[8,640,128]{2,1,0:T(8,128)(2,1)}, u32[]{:S(2)}, u32[]{:S(2)}) collective-permute-start(bf16[8,640,128]{2,1,0:T(8,128)(2,1)} %collective-permute-done.8.refs_2_), channel_id=1, source_target_pairs={{0,3},{1,0},{2,1},{3,2},{4,7},{5,4},{6,5},{7,6},{8,11},{9,8},{10,9... | collective-permute-start | bytes 3932168 | tf_op jit(solution)/shard_map/ppermute | solution.py:37
  79.3 9.6 %transform.4 = (bf16[4,2,128,128]{3,2,1,0:T(8,128)(2,1)S(1)}, bf16[4,2,128,128]{3,2,1,0:T(8,128)(2,1)S(1)}, bf16[4,2,128,128]{3,2,1,0:T(8,128)(2,1)S(1)}, bf16[4...) custom-call(s32[8,128]{1,0:T(8,128)S(1)} %notes.1.codes, ...), custom_call_target="tpu_custom_call" | custom-call | flops 6442450944 | bytes 16777216 | tf_op jit(solution)/shard_map/transform/pallas_call | solution.py:154
  89.0 4.3 %collective-permute-start.13 = (bf16[4,2,128,128]{3,2,1,0:T(8,128)(2,1)S(1)}, bf16[4,2,128,128]{3,2,1,0:T(8,128)(2,1)S(1)}, u32[]{:S(2)}, u32[]{:S(2)}) collective-permute-start(bf16[4,2,128,128]{3,2,1,0:T(8,128)(2,1)S(1)} %get-tuple-element.98), channel_id=1, source_target_pairs={{0,64},{16,80},{32,96},{48,112},{64,0},{80,16},{96,32},{112,48},{1... | collective-permute-start | bytes 786440 | tf_op jit(solution)/shard_map/ppermute | solution.py:42
  96.0 9.9 %collective-permute-done.31.refs_1_ = bf16[8,640,128]{2,1,0:T(8,128)(2,1)} collective-permute-done((bf16[8,640,128]{2,1,0:T(8,128)(2,1)}, bf16[8,640,128]{2,1,0:T(8,128)(2,1)}, u32[]{:S(2)}, u32[]{:S(2)}) %collective-permute-start.31) | collective-permute-done | bytes 1310752 | tf_op jit(solution)/shard_map/ppermute | solution.py:37
  107.4 2.3 collective-permute-start.18
  109.7 2.4 collective-permute-start.32
  112.1 9.6 %transform.5 = (bf16[4,2,128,128]{3,2,1,0:T(8,128)(2,1)S(1)}, bf16[4,2,128,128]{3,2,1,0:T(8,128)(2,1)S(1)}, bf16[4,2,128,128]{3,2,1,0:T(8,128)(2,1)S(1)}, bf16[4...) custom-call(s32[8,128]{1,0:T(8,128)S(1)} %notes.1.codes, ...), custom_call_target="tpu_custom_call" | custom-call | flops 6442450944 | bytes 16777216 | tf_op jit(solution)/shard_map/transform/pallas_call | solution.py:154
  125.6 10.4 %collective-permute-done.23.refs_1_ = bf16[4,2,128,128]{3,2,1,0:T(8,128)(2,1)S(1)} collective-permute-done((bf16[4,2,128,128]{3,2,1,0:T(8,128)(2,1)S(1)}, bf16[4,2,128,128]{3,2,1,0:T(8,128)(2,1)S(1)}, u32[]{:S(2)}, u32[]{:S(2)}) %collective-permute-start.23) | collective-permute-done | bytes 262176 | tf_op jit(solution)/shard_map/ppermute | solution.py:42
  139.4 11.4 %collective-permute-done.27.refs_5_ = bf16[4,2,128,128]{3,2,1,0:T(8,128)(2,1)S(1)} collective-permute-done((bf16[4,2,128,128]{3,2,1,0:T(8,128)(2,1)S(1)}, bf16[4,2,128,128]{3,2,1,0:T(8,128)(2,1)S(1)}, u32[]{:S(2)}, u32[]{:S(2)}) %collective-permute-start.27) | collective-permute-done | bytes 262176 | tf_op jit(solution)/shard_map/ppermute | solution.py:42
  150.9 3.1 %collective-permute-start.36 = (bf16[8,640,128]{2,1,0:T(8,128)(2,1)}, bf16[8,640,128]{2,1,0:T(8,128)(2,1)S(1)}, u32[]{:S(2)}, u32[]{:S(2)}) collective-permute-start(bf16[8,640,128]{2,1,0:T(8,128)(2,1)} %collective-permute-done.20.refs_1_), channel_id=1, source_target_pairs={{0,1},{1,2},{2,3},{3,0},{4,5},{5,6},{6,7},{7,4},{8,9},{9,10},{10,1... | collective-permute-start | bytes 3932168 | tf_op jit(solution)/shard_map/ppermute | solution.py:37
  154.1 4.2 %cycle.4.refs_8_ = f32[8,128,128]{2,1,0:T(8,128)S(1)} custom-call(s32[256]{0:T(256)S(1)} %bitcast.10, s32[2]{0:T(128)S(1)} %pad_add_fusion.me, bf16[256,128,128]{2,1,0:T(8,128)(2,1)S(1)} %bitcast.6, bf16[4,2,128,128]{3,2,1,0:T(8,128)(2,1)S(1)} %get-tuple-element.96.refs_0_, bf16[4,2,128,128]{3,2,1,0:T(8,128)(2,1)S(1)} %collective-permute-done.12.refs_1_, ...), custom_call_target="tpu_custom_call" | custom-call | flops 2147483648 | bytes 6291456 | tf_op jit(solution)/shard_map/cycle/pallas_call | solution.py:212
  158.3 9.3 %transform.6 = (bf16[4,2,128,128]{3,2,1,0:T(8,128)(2,1)S(1)}, bf16[4,2,128,128]{3,2,1,0:T(8,128)(2,1)S(1)}, bf16[4,2,128,128]{3,2,1,0:T(8,128)(2,1)S(1)}, bf16[4...) custom-call(s32[8,128]{1,0:T(8,128)S(1)} %notes.1.codes, ...), custom_call_target="tpu_custom_call" | custom-call | flops 6442450944 | bytes 16777216 | tf_op jit(solution)/shard_map/transform/pallas_call | solution.py:154
  167.6 4.2 %cycle.5.refs_8_ = f32[8,128,128]{2,1,0:T(8,128)S(1)} custom-call(s32[256]{0:T(256)S(1)} %bitcast.11, s32[2]{0:T(128)S(1)} %pad_add_fusion.me, bf16[256,128,128]{2,1,0:T(8,128)(2,1)S(1)} %bitcast.7, bf16[4,2,128,128]{3,2,1,0:T(8,128)(2,1)S(1)} %get-tuple-element.115.refs_0_, bf16[4,2,128,128]{3,2,1,0:T(8,128)(2,1)S(1)} %collective-permute-done.23.refs_1_, ...), custom_call_target="tpu_custom_call" | custom-call | flops 2147483648 | bytes 6291456 | tf_op jit(solution)/shard_map/cycle/pallas_call | solution.py:212
  173.9 2.3 collective-permute-start.47
  176.2 7.6 %collective-permute-done.37.refs_3_ = bf16[8,640,128]{2,1,0:T(8,128)(2,1)S(1)} collective-permute-done((bf16[8,640,128]{2,1,0:T(8,128)(2,1)S(1)}, bf16[8,640,128]{2,1,0:T(8,128)(2,1)S(1)}, u32[]{:S(2)}, u32[]{:S(2)}) %collective-permute-start.37) | collective-permute-done | bytes 1310752 | tf_op jit(solution)/shard_map/ppermute | solution.py:37
  183.8 7.9 %transform.7 = (bf16[4,2,128,128]{3,2,1,0:T(8,128)(2,1)S(1)}, bf16[4,2,128,128]{3,2,1,0:T(8,128)(2,1)S(1)}, bf16[4,2,128,128]{3,2,1,0:T(8,128)(2,1)S(1)}, bf16[4...) custom-call(s32[8,128]{1,0:T(8,128)S(1)} %notes.1.codes, ...), custom_call_target="tpu_custom_call" | custom-call | flops 6442450944 | bytes 16777216 | tf_op jit(solution)/shard_map/transform/pallas_call | solution.py:154
  197.1 2.5 %collective-permute-start.40 = (bf16[4,2,128,128]{3,2,1,0:T(8,128)(2,1)S(1)}, bf16[4,2,128,128]{3,2,1,0:T(8,128)(2,1)S(1)}, u32[]{:S(2)}, u32[]{:S(2)}) collective-permute-start(bf16[4,2,128,128]{3,2,1,0:T(8,128)(2,1)S(1)} %get-tuple-element.146), channel_id=1, source_target_pairs={{0,96},{16,112},{32,0},{48,16},{64,32},{80,48},{96,64},{112,80},{1... | collective-permute-start | bytes 786440 | tf_op jit(solution)/shard_map/ppermute | solution.py:42
  199.6 2.4 collective-permute-done.50.refs_6_
  201.9 5.0 %collective-permute-done.51.refs_7_ = bf16[4,2,128,128]{3,2,1,0:T(8,128)(2,1)S(1)} collective-permute-done((bf16[4,2,128,128]{3,2,1,0:T(8,128)(2,1)S(1)}, bf16[4,2,128,128]{3,2,1,0:T(8,128)(2,1)S(1)}, u32[]{:S(2)}, u32[]{:S(2)}) %collective-permute-start.51) | collective-permute-done | bytes 262176 | tf_op jit(solution)/shard_map/ppermute | solution.py:42
  207.7 5.3 %collective-permute-start.43 = (bf16[4,2,128,128]{3,2,1,0:T(8,128)(2,1)S(1)}, bf16[4,2,128,128]{3,2,1,0:T(8,128)(2,1)S(1)}, u32[]{:S(2)}, u32[]{:S(2)}) collective-permute-start(bf16[4,2,128,128]{3,2,1,0:T(8,128)(2,1)S(1)} %get-tuple-element.149), channel_id=1, source_target_pairs={{0,80},{16,64},{32,112},{48,96},{64,16},{80,0},{96,48},{112,32},{1... | collective-permute-start | bytes 786440 | tf_op jit(solution)/shard_map/ppermute | solution.py:42
  214.4 4.2 %cycle.6.refs_8_ = f32[8,128,128]{2,1,0:T(8,128)S(1)} custom-call(s32[256]{0:T(256)S(1)} %bitcast.12, s32[2]{0:T(128)S(1)} %pad_add_fusion.me, bf16[256,128,128]{2,1,0:T(8,128)(2,1)S(1)} %bitcast.8, bf16[4,2,128,128]{3,2,1,0:T(8,128)(2,1)S(1)} %get-tuple-element.151.refs_0_, bf16[4,2,128,128]{3,2,1,0:T(8,128)(2,1)S(1)} %collective-permute-done.45.refs_1_, ...), custom_call_target="tpu_custom_call" | custom-call | flops 2147483648 | bytes 6291456 | tf_op jit(solution)/shard_map/cycle/pallas_call | solution.py:212
  219.7 3.8 %collective-permute-done.43.refs_6_ = bf16[4,2,128,128]{3,2,1,0:T(8,128)(2,1)S(1)} collective-permute-done((bf16[4,2,128,128]{3,2,1,0:T(8,128)(2,1)S(1)}, bf16[4,2,128,128]{3,2,1,0:T(8,128)(2,1)S(1)}, u32[]{:S(2)}, u32[]{:S(2)}) %collective-permute-start.43) | collective-permute-done | bytes 262176 | tf_op jit(solution)/shard_map/ppermute | solution.py:42
  223.4 5.5 %collective-permute-done.44.refs_7_ = bf16[4,2,128,128]{3,2,1,0:T(8,128)(2,1)S(1)} collective-permute-done((bf16[4,2,128,128]{3,2,1,0:T(8,128)(2,1)S(1)}, bf16[4,2,128,128]{3,2,1,0:T(8,128)(2,1)S(1)}, u32[]{:S(2)}, u32[]{:S(2)}) %collective-permute-start.44) | collective-permute-done | bytes 262176 | tf_op jit(solution)/shard_map/ppermute | solution.py:42
  228.9 4.2 %cycle.7.own = bf16[8,128,128]{2,1,0:T(8,128)(2,1)S(1)} custom-call(s32[256]{0:T(256)S(1)} %bitcast.13, s32[2]{0:T(128)S(1)} %pad_add_fusion.me, bf16[256,128,128]{2,1,0:T(8,128)(2,1)S(1)} %bitcast.9, bf16[4,2,128,128]{3,2,1,0:T(8,128)(2,1)S(1)} %get-tuple-element.143.refs_0_, bf16[4,2,128,128]{3,2,1,0:T(8,128)(2,1)S(1)} %collective-permute-done.38.refs_1_, ...), custom_call_target="tpu_custom_call" | custom-call | flops 2147483648 | bytes 6291456 | tf_op jit(solution)/shard_map/cycle/pallas_call | solution.py:212
  233.3 10.5 %collective-permute-done.52.partner = bf16[8,128,128]{2,1,0:T(8,128)(2,1)S(1)} collective-permute-done((bf16[8,128,128]{2,1,0:T(8,128)(2,1)S(1)}, bf16[8,128,128]{2,1,0:T(8,128)(2,1)S(1)}, u32[]{:S(2)}, u32[]{:S(2)}) %collective-permute-start.52) | collective-permute-done | bytes 262176 | tf_op jit(solution)/shard_map/ppermute | solution.py:454
  (154 shorter events, 50.6 us)
Async XLA Ops:
  8.0 25.8 %collective-permute-start = (bf16[1040,512]{1,0:T(8,128)(2,1)S(1)}, bf16[1040,512]{1,0:T(8,128)(2,1)S(1)}, u32[]{:S(2)}, u32[]{:S(2)}) collective-permute-start(bf16[1040,512]{1,0:T(8,128)(2,1)S(1)} %get-tuple-element.83.refs_0_.refs_4_.refs_5_), channel_id=1, source_target_pairs={{0,96},{16,112},{32,0},{48,16},{64,32},{80,48},{96,64},{112,80},{1... | collective-permute-start | bytes 3194888 | tf_op jit(solution)/shard_map/ppermute | solution.py:42
  11.0 26.6 %collective-permute-start.2 = (bf16[1040,512]{1,0:T(8,128)(2,1)S(1)}, bf16[1040,512]{1,0:T(8,128)(2,1)S(1)}, u32[]{:S(2)}, u32[]{:S(2)}) collective-permute-start(bf16[1040,512]{1,0:T(8,128)(2,1)S(1)} %get-tuple-element.83.refs_0_.refs_4_.refs_5_), channel_id=1, source_target_pairs={{0,32},{16,48},{32,64},{48,80},{64,96},{80,112},{96,0},{112,16},{1... | collective-permute-start | bytes 3194888 | tf_op jit(solution)/shard_map/ppermute | solution.py:42
  11.0 26.7 %collective-permute-start.7 = (bf16[8,640,128]{2,1,0:T(8,128)(2,1)}, bf16[8,640,128]{2,1,0:T(8,128)(2,1)}, u32[]{:S(2)}, u32[]{:S(2)}) collective-permute-start(bf16[8,640,128]{2,1,0:T(8,128)(2,1)} %get-tuple-element.87.refs_0_), channel_id=1, source_target_pairs={{0,12},{1,13},{2,14},{3,15},{4,0},{5,1},{6,2},{7,3},{8,4},{9,5},{1... | collective-permute-start | bytes 3932168 | tf_op jit(solution)/shard_map/ppermute | solution.py:37
  11.8 25.9 %collective-permute-start.8 = (bf16[8,640,128]{2,1,0:T(8,128)(2,1)}, bf16[8,640,128]{2,1,0:T(8,128)(2,1)}, u32[]{:S(2)}, u32[]{:S(2)}) collective-permute-start(bf16[8,640,128]{2,1,0:T(8,128)(2,1)} %get-tuple-element.87.refs_0_), channel_id=1, source_target_pairs={{0,4},{1,5},{2,6},{3,7},{4,8},{5,9},{6,10},{7,11},{8,12},{9,13},{1... | collective-permute-start | bytes 3932168 | tf_op jit(solution)/shard_map/ppermute | solution.py:37
  14.2 25.0 %collective-permute-start.3 = (bf16[1040,512]{1,0:T(8,128)(2,1)S(1)}, bf16[1040,512]{1,0:T(8,128)(2,1)S(1)}, u32[]{:S(2)}, u32[]{:S(2)}) collective-permute-start(bf16[1040,512]{1,0:T(8,128)(2,1)S(1)} %get-tuple-element.83.refs_0_.refs_4_.refs_5_), channel_id=1, source_target_pairs={{0,16},{16,0},{32,48},{48,32},{64,80},{80,64},{96,112},{112,96},{1... | collective-permute-start | bytes 3194888 | tf_op jit(solution)/shard_map/ppermute | solution.py:42
  33.8 17.6 %collective-permute-start.1 = (bf16[528,512]{1,0:T(8,128)(2,1)S(1)}, bf16[528,512]{1,0:T(8,128)(2,1)S(1)}, u32[]{:S(2)}, u32[]{:S(2)}) collective-permute-start(bf16[528,512]{1,0:T(8,128)(2,1)S(1)} %slice.8), channel_id=1, source_target_pairs={{0,96},{16,112},{32,0},{48,16},{64,32},{80,48},{96,64},{112,80},{1... | collective-permute-start | bytes 1622024 | tf_op jit(solution)/shard_map/ppermute | solution.py:42
  37.7 24.2 %collective-permute-start.22 = (bf16[8,640,128]{2,1,0:T(8,128)(2,1)}, bf16[8,640,128]{2,1,0:T(8,128)(2,1)S(1)}, u32[]{:S(2)}, u32[]{:S(2)}) collective-permute-start(bf16[8,640,128]{2,1,0:T(8,128)(2,1)} %get-tuple-element.87.refs_0_), channel_id=1, source_target_pairs={{0,8},{1,9},{2,10},{3,11},{4,12},{5,13},{6,14},{7,15},{8,0},{9,1},... | collective-permute-start | bytes 3932168 | tf_op jit(solution)/shard_map/ppermute | solution.py:37
  39.2 26.8 %collective-permute-start.9 = (bf16[8,640,128]{2,1,0:T(8,128)(2,1)}, bf16[8,640,128]{2,1,0:T(8,128)(2,1)S(1)}, u32[]{:S(2)}, u32[]{:S(2)}) collective-permute-start(bf16[8,640,128]{2,1,0:T(8,128)(2,1)} %get-tuple-element.87.refs_0_), channel_id=1, source_target_pairs={{0,1},{1,2},{2,3},{3,0},{4,5},{5,6},{6,7},{7,4},{8,9},{9,10},{10,1... | collective-permute-start | bytes 3932168 | tf_op jit(solution)/shard_map/ppermute | solution.py:37
  40.2 16.4 %collective-permute-start.4 = (bf16[1040,512]{1,0:T(8,128)(2,1)S(1)}, bf16[1040,512]{1,0:T(8,128)(2,1)S(1)}, u32[]{:S(2)}, u32[]{:S(2)}) collective-permute-start(bf16[1040,512]{1,0:T(8,128)(2,1)S(1)} %collective-permute-done.refs_1_.refs_6_.refs_7_), channel_id=1, source_target_pairs={{0,16},{16,0},{32,48},{48,32},{64,80},{80,64},{96,112},{112,96},{1... | collective-permute-start | bytes 3194888 | tf_op jit(solution)/shard_map/ppermute | solution.py:42
  57.6 31.3 %collective-permute-start.20 = (bf16[8,640,128]{2,1,0:T(8,128)(2,1)}, bf16[8,640,128]{2,1,0:T(8,128)(2,1)}, u32[]{:S(2)}, u32[]{:S(2)}) collective-permute-start(bf16[8,640,128]{2,1,0:T(8,128)(2,1)} %collective-permute-done.8.refs_2_), channel_id=1, source_target_pairs={{0,1},{1,2},{2,3},{3,0},{4,5},{5,6},{6,7},{7,4},{8,9},{9,10},{10,1... | collective-permute-start | bytes 3932168 | tf_op jit(solution)/shard_map/ppermute | solution.py:37
  58.6 30.4 %collective-permute-start.21 = (bf16[8,640,128]{2,1,0:T(8,128)(2,1)}, bf16[8,640,128]{2,1,0:T(8,128)(2,1)}, u32[]{:S(2)}, u32[]{:S(2)}) collective-permute-start(bf16[8,640,128]{2,1,0:T(8,128)(2,1)} %collective-permute-done.7.refs_1_), channel_id=1, source_target_pairs={{0,3},{1,0},{2,1},{3,2},{4,7},{5,4},{6,5},{7,6},{8,11},{9,8},{10,9... | collective-permute-start | bytes 3932168 | tf_op jit(solution)/shard_map/ppermute | solution.py:37
  61.5 31.8 %collective-permute-start.19 = (bf16[8,640,128]{2,1,0:T(8,128)(2,1)}, bf16[8,640,128]{2,1,0:T(8,128)(2,1)}, u32[]{:S(2)}, u32[]{:S(2)}) collective-permute-start(bf16[8,640,128]{2,1,0:T(8,128)(2,1)} %get-tuple-element.87.refs_0_), channel_id=1, source_target_pairs={{0,3},{1,0},{2,1},{3,2},{4,7},{5,4},{6,5},{7,6},{8,11},{9,8},{10,9... | collective-permute-start | bytes 3932168 | tf_op jit(solution)/shard_map/ppermute | solution.py:37
  61.9 32.4 %collective-permute-start.30 = (bf16[8,640,128]{2,1,0:T(8,128)(2,1)}, bf16[8,640,128]{2,1,0:T(8,128)(2,1)}, u32[]{:S(2)}, u32[]{:S(2)}) collective-permute-start(bf16[8,640,128]{2,1,0:T(8,128)(2,1)} %collective-permute-done.7.refs_1_), channel_id=1, source_target_pairs={{0,1},{1,2},{2,3},{3,0},{4,5},{5,6},{6,7},{7,4},{8,9},{9,10},{10,1... | collective-permute-start | bytes 3932168 | tf_op jit(solution)/shard_map/ppermute | solution.py:37
  67.1 38.7 %collective-permute-start.31 = (bf16[8,640,128]{2,1,0:T(8,128)(2,1)}, bf16[8,640,128]{2,1,0:T(8,128)(2,1)}, u32[]{:S(2)}, u32[]{:S(2)}) collective-permute-start(bf16[8,640,128]{2,1,0:T(8,128)(2,1)} %collective-permute-done.8.refs_2_), channel_id=1, source_target_pairs={{0,3},{1,0},{2,1},{3,2},{4,7},{5,4},{6,5},{7,6},{8,11},{9,8},{10,9... | collective-permute-start | bytes 3932168 | tf_op jit(solution)/shard_map/ppermute | solution.py:37
  88.9 17.7 %collective-permute-start.12 = (bf16[4,2,128,128]{3,2,1,0:T(8,128)(2,1)S(1)}, bf16[4,2,128,128]{3,2,1,0:T(8,128)(2,1)S(1)}, u32[]{:S(2)}, u32[]{:S(2)}) collective-permute-start(bf16[4,2,128,128]{3,2,1,0:T(8,128)(2,1)S(1)} %get-tuple-element.97), channel_id=1, source_target_pairs={{0,32},{16,48},{32,64},{48,80},{64,96},{80,112},{96,0},{112,16},{1... | collective-permute-start | bytes 786440 | tf_op jit(solution)/shard_map/ppermute | solution.py:42
  89.0 17.6 %collective-permute-start.13 = (bf16[4,2,128,128]{3,2,1,0:T(8,128)(2,1)S(1)}, bf16[4,2,128,128]{3,2,1,0:T(8,128)(2,1)S(1)}, u32[]{:S(2)}, u32[]{:S(2)}) collective-permute-start(bf16[4,2,128,128]{3,2,1,0:T(8,128)(2,1)S(1)} %get-tuple-element.98), channel_id=1, source_target_pairs={{0,64},{16,80},{32,96},{48,112},{64,0},{80,16},{96,32},{112,48},{1... | collective-permute-start | bytes 786440 | tf_op jit(solution)/shard_map/ppermute | solution.py:42
  105.8 48.2 %collective-permute-start.33 = (bf16[8,640,128]{2,1,0:T(8,128)(2,1)S(1)}, bf16[8,640,128]{2,1,0:T(8,128)(2,1)S(1)}, u32[]{:S(2)}, u32[]{:S(2)}) collective-permute-start(bf16[8,640,128]{2,1,0:T(8,128)(2,1)S(1)} %copy-done.23), channel_id=1, source_target_pairs={{0,3},{1,0},{2,1},{3,2},{4,7},{5,4},{6,5},{7,6},{8,11},{9,8},{10,9... | collective-permute-start | bytes 3932168 | tf_op jit(solution)/shard_map/ppermute | solution.py:37
  106.7 16.2 %collective-permute-start.17 = (bf16[4,2,128,128]{3,2,1,0:T(8,128)(2,1)S(1)}, bf16[4,2,128,128]{3,2,1,0:T(8,128)(2,1)S(1)}, u32[]{:S(2)}, u32[]{:S(2)}) collective-permute-start(bf16[4,2,128,128]{3,2,1,0:T(8,128)(2,1)S(1)} %get-tuple-element.102), channel_id=1, source_target_pairs={{0,80},{16,64},{32,112},{48,96},{64,16},{80,0},{96,48},{112,32},{1... | collective-permute-start | bytes 786440 | tf_op jit(solution)/shard_map/ppermute | solution.py:42
  107.4 16.8 %collective-permute-start.18 = (bf16[4,2,128,128]{3,2,1,0:T(8,128)(2,1)S(1)}, bf16[4,2,128,128]{3,2,1,0:T(8,128)(2,1)S(1)}, u32[]{:S(2)}, u32[]{:S(2)}) collective-permute-start(bf16[4,2,128,128]{3,2,1,0:T(8,128)(2,1)S(1)} %get-tuple-element.103), channel_id=1, source_target_pairs={{0,112},{16,96},{32,16},{48,0},{64,48},{80,32},{96,80},{112,64},{1... | collective-permute-start | bytes 786440 | tf_op jit(solution)/shard_map/ppermute | solution.py:42
  109.7 48.5 %collective-permute-start.32 = (bf16[8,640,128]{2,1,0:T(8,128)(2,1)S(1)}, bf16[8,640,128]{2,1,0:T(8,128)(2,1)S(1)}, u32[]{:S(2)}, u32[]{:S(2)}) collective-permute-start(bf16[8,640,128]{2,1,0:T(8,128)(2,1)S(1)} %copy-done.23), channel_id=1, source_target_pairs={{0,1},{1,2},{2,3},{3,0},{4,5},{5,6},{6,7},{7,4},{8,9},{9,10},{10,1... | collective-permute-start | bytes 3932168 | tf_op jit(solution)/shard_map/ppermute | solution.py:37
  137.5 35.9 %collective-permute-start.34 = (bf16[8,640,128]{2,1,0:T(8,128)(2,1)S(1)}, bf16[8,640,128]{2,1,0:T(8,128)(2,1)S(1)}, u32[]{:S(2)}, u32[]{:S(2)}) collective-permute-start(bf16[8,640,128]{2,1,0:T(8,128)(2,1)S(1)} %copy-done.21), channel_id=1, source_target_pairs={{0,1},{1,2},{2,3},{3,0},{4,5},{5,6},{6,7},{7,4},{8,9},{9,10},{10,1... | collective-permute-start | bytes 3932168 | tf_op jit(solution)/shard_map/ppermute | solution.py:37
  150.8 23.1 %collective-permute-start.35 = (bf16[8,640,128]{2,1,0:T(8,128)(2,1)}, bf16[8,640,128]{2,1,0:T(8,128)(2,1)S(1)}, u32[]{:S(2)}, u32[]{:S(2)}) collective-permute-start(bf16[8,640,128]{2,1,0:T(8,128)(2,1)} %collective-permute-done.21.refs_2_), channel_id=1, source_target_pairs={{0,3},{1,0},{2,1},{3,2},{4,7},{5,4},{6,5},{7,6},{8,11},{9,8},{10,9... | collective-permute-start | bytes 3932168 | tf_op jit(solution)/shard_map/ppermute | solution.py:37
  150.9 25.3 %collective-permute-start.36 = (bf16[8,640,128]{2,1,0:T(8,128)(2,1)}, bf16[8,640,128]{2,1,0:T(8,128)(2,1)S(1)}, u32[]{:S(2)}, u32[]{:S(2)}) collective-permute-start(bf16[8,640,128]{2,1,0:T(8,128)(2,1)} %collective-permute-done.20.refs_1_), channel_id=1, source_target_pairs={{0,1},{1,2},{2,3},{3,0},{4,5},{5,6},{6,7},{7,4},{8,9},{9,10},{10,1... | collective-permute-start | bytes 3932168 | tf_op jit(solution)/shard_map/ppermute | solution.py:37
  154.0 29.8 %collective-permute-start.37 = (bf16[8,640,128]{2,1,0:T(8,128)(2,1)S(1)}, bf16[8,640,128]{2,1,0:T(8,128)(2,1)S(1)}, u32[]{:S(2)}, u32[]{:S(2)}) collective-permute-start(bf16[8,640,128]{2,1,0:T(8,128)(2,1)S(1)} %collective-permute-done.33.refs_3_), channel_id=1, source_target_pairs={{0,3},{1,0},{2,1},{3,2},{4,7},{5,4},{6,5},{7,6},{8,11},{9,8},{10,9... | collective-permute-start | bytes 3932168 | tf_op jit(solution)/shard_map/ppermute | solution.py:37
  171.8 19.9 %collective-permute-start.45 = (bf16[4,2,128,128]{3,2,1,0:T(8,128)(2,1)S(1)}, bf16[4,2,128,128]{3,2,1,0:T(8,128)(2,1)S(1)}, u32[]{:S(2)}, u32[]{:S(2)}) collective-permute-start(bf16[4,2,128,128]{3,2,1,0:T(8,128)(2,1)S(1)} %get-tuple-element.152), channel_id=1, source_target_pairs={{0,32},{16,48},{32,64},{48,80},{64,96},{80,112},{96,0},{112,16},{1... | collective-permute-start | bytes 786440 | tf_op jit(solution)/shard_map/ppermute | solution.py:42
  173.4 19.8 %collective-permute-start.46 = (bf16[4,2,128,128]{3,2,1,0:T(8,128)(2,1)S(1)}, bf16[4,2,128,128]{3,2,1,0:T(8,128)(2,1)S(1)}, u32[]{:S(2)}, u32[]{:S(2)}) collective-permute-start(bf16[4,2,128,128]{3,2,1,0:T(8,128)(2,1)S(1)} %get-tuple-element.153), channel_id=1, source_target_pairs={{0,64},{16,80},{32,96},{48,112},{64,0},{80,16},{96,32},{112,48},{1... | collective-permute-start | bytes 786440 | tf_op jit(solution)/shard_map/ppermute | solution.py:42
  173.9 21.0 %collective-permute-start.47 = (bf16[4,2,128,128]{3,2,1,0:T(8,128)(2,1)S(1)}, bf16[4,2,128,128]{3,2,1,0:T(8,128)(2,1)S(1)}, u32[]{:S(2)}, u32[]{:S(2)}) collective-permute-start(bf16[4,2,128,128]{3,2,1,0:T(8,128)(2,1)S(1)} %get-tuple-element.154), channel_id=1, source_target_pairs={{0,96},{16,112},{32,0},{48,16},{64,32},{80,48},{96,64},{112,80},{1... | collective-permute-start | bytes 786440 | tf_op jit(solution)/shard_map/ppermute | solution.py:42
  176.2 19.5 %collective-permute-start.48 = (bf16[4,2,128,128]{3,2,1,0:T(8,128)(2,1)S(1)}, bf16[4,2,128,128]{3,2,1,0:T(8,128)(2,1)S(1)}, u32[]{:S(2)}, u32[]{:S(2)}) collective-permute-start(bf16[4,2,128,128]{3,2,1,0:T(8,128)(2,1)S(1)} %get-tuple-element.155), channel_id=1, source_target_pairs={{0,16},{16,0},{32,48},{48,32},{64,80},{80,64},{96,112},{112,96},{1... | collective-permute-start | bytes 786440 | tf_op jit(solution)/shard_map/ppermute | solution.py:42
  195.7 17.3 %collective-permute-start.39 = (bf16[4,2,128,128]{3,2,1,0:T(8,128)(2,1)S(1)}, bf16[4,2,128,128]{3,2,1,0:T(8,128)(2,1)S(1)}, u32[]{:S(2)}, u32[]{:S(2)}) collective-permute-start(bf16[4,2,128,128]{3,2,1,0:T(8,128)(2,1)S(1)} %get-tuple-element.145), channel_id=1, source_target_pairs={{0,64},{16,80},{32,96},{48,112},{64,0},{80,16},{96,32},{112,48},{1... | collective-permute-start | bytes 786440 | tf_op jit(solution)/shard_map/ppermute | solution.py:42
  197.1 22.6 %collective-permute-start.40 = (bf16[4,2,128,128]{3,2,1,0:T(8,128)(2,1)S(1)}, bf16[4,2,128,128]{3,2,1,0:T(8,128)(2,1)S(1)}, u32[]{:S(2)}, u32[]{:S(2)}) collective-permute-start(bf16[4,2,128,128]{3,2,1,0:T(8,128)(2,1)S(1)} %get-tuple-element.146), channel_id=1, source_target_pairs={{0,96},{16,112},{32,0},{48,16},{64,32},{80,48},{96,64},{112,80},{1... | collective-permute-start | bytes 786440 | tf_op jit(solution)/shard_map/ppermute | solution.py:42
  201.9 17.7 %collective-permute-start.41 = (bf16[4,2,128,128]{3,2,1,0:T(8,128)(2,1)S(1)}, bf16[4,2,128,128]{3,2,1,0:T(8,128)(2,1)S(1)}, u32[]{:S(2)}, u32[]{:S(2)}) collective-permute-start(bf16[4,2,128,128]{3,2,1,0:T(8,128)(2,1)S(1)} %get-tuple-element.147), channel_id=1, source_target_pairs={{0,16},{16,0},{32,48},{48,32},{64,80},{80,64},{96,112},{112,96},{1... | collective-permute-start | bytes 786440 | tf_op jit(solution)/shard_map/ppermute | solution.py:42
  213.0 16.0 %collective-permute-start.44 = (bf16[4,2,128,128]{3,2,1,0:T(8,128)(2,1)S(1)}, bf16[4,2,128,128]{3,2,1,0:T(8,128)(2,1)S(1)}, u32[]{:S(2)}, u32[]{:S(2)}) collective-permute-start(bf16[4,2,128,128]{3,2,1,0:T(8,128)(2,1)S(1)} %get-tuple-element.150), channel_id=1, source_target_pairs={{0,112},{16,96},{32,16},{48,0},{64,48},{80,32},{96,80},{112,64},{1... | collective-permute-start | bytes 786440 | tf_op jit(solution)/shard_map/ppermute | solution.py:42
  (52 other events, 548.4 us)

commit v2 on v1

--- a/solution.py
+++ b/solution.py
@@ -172,30 +172,31 @@
     )(codes, me, *blocks, *[line for line, _ in lines])
 
 
-def cycle_kernel(chunk, spots, me, cycle, *refs):
-    arrived, before, total = refs[:8], refs[8], refs[9]
-    values, sums, sems = refs[10:]
+def cycle_kernel(chunk, readers, spots, me, cycle, *refs):
+    number = len(readers)
+    arrived, before, total = refs[:number], refs[number], refs[number + 1]
+    values, sums, sems = refs[number + 2 :]
     i, j = me[0], me[1]
     y, core = i >> 1, i & 1
     x, z = j >> 2, j & 3
 
     copies = [
-        pltpu.make_async_copy(arrived[r], values.at[r], sems.at[r]) for r in range(8)
+        pltpu.make_async_copy(arrived[k], values.at[k], sems.at[k]) for k in range(number)
     ]
     for copy in copies:
         copy.start()
     sums[...] = before[...]
-    for r in range(8):
+    for k, r in enumerate(readers):
         other = core ^ (r >> 2)
         worker = ((y - (r & 3)) & 3) * 2 + other
-        copies[r].wait()
+        copies[k].wait()
         parts = []
         for n, (u, t) in enumerate(chunk):
             owner = worker * 16 + owner_ja(other, x, z, u, t)
             for h in range(2):
                 spot = spots[h * 128 + owner]
                 block = cycle[spot]
-                value = values[r, n, h]
+                value = values[k, n, h]
                 part = jnp.dot(block, value, preferred_element_type=jnp.float32)
                 part += lax.dot_general(value, block, NT, preferred_element_type=jnp.float32)
                 parts.append((spot >> 5, part))
@@ -204,27 +205,27 @@
     total[...] = sums[...].astype(total.dtype)
 
 
-def cycle_part(chunk, spots, me, cycle, arrived, before, dtype):
+def cycle_part(chunk, spots, me, cycle, arrived, before, dtype, readers=tuple(range(8))):
     smem = pl.BlockSpec(memory_space=pltpu.SMEM)
     vmem = pl.BlockSpec(memory_space=pltpu.VMEM)
     hbm = pl.BlockSpec(memory_space=pltpu.HBM)
     width = cycle.shape[-1]
     return pl.pallas_call(
-        functools.partial(cycle_kernel, chunk),
+        functools.partial(cycle_kernel, chunk, readers),
         out_shape=jax.ShapeDtypeStruct(before.shape, dtype),
-        in_specs=[smem, smem, vmem] + [hbm] * 8 + [vmem],
+        in_specs=[smem, smem, vmem] + [hbm] * len(readers) + [vmem],
         out_specs=vmem,
         scratch_shapes=[
-            pltpu.VMEM((8,) + arrived[0].shape, jnp.bfloat16),
+            pltpu.VMEM((len(readers),) + arrived[0].shape, jnp.bfloat16),
             pltpu.VMEM(before.shape, jnp.float32),
-            pltpu.SemaphoreType.DMA((8,)),
+            pltpu.SemaphoreType.DMA((len(readers),)),
         ],
         compiler_params=pltpu.CompilerParams(vmem_limit_bytes=20 << 20),
         cost_estimate=pl.CostEstimate(
-            flops=4 * 64 * 4 * width**3, bytes_accessed=6 << 20, transcendentals=0
+            flops=4 * 8 * len(readers) * 4 * width**3, bytes_accessed=6 << 20, transcendentals=0
         ),
         name="cycle",
-    )(spots, me, cycle, *arrived, before)
+    )(spots, me, cycle, *[arrived[r] for r in readers], before)
 
 
 def prep_kernel(count, entries, amps, bases, block, line, masked, spots):
@@ -432,9 +433,7 @@
     arrivals = []
     for c, chunk in enumerate(CHUNKS):
         if c >= 2:
-            total = cycle_part(
-                CHUNKS[c - 2], spots, me, cycle, arrivals[c - 2], total, jnp.float32
-            )
+            total = cycle_part(CHUNKS[c - 2], spots, me, cycle, arrivals[c - 2], total, jnp.float32)
             codes, total = lax.optimization_barrier((codes, total))
         sent = transform(chunk, codes, me, [held[key] for key in chunk], lines)
         sent, total = lax.optimization_barrier((sent, total))
@@ -449,7 +448,10 @@
             back.append(shift_ia(sent[r], r & 3, r >> 2))
         arrivals.append(back)
     total = cycle_part(CHUNKS[2], spots, me, cycle, arrivals[2], total, jnp.float32)
-    cycle_sum = cycle_part(CHUNKS[3], spots, me, cycle, arrivals[3], total, jnp.bfloat16)
+    total = cycle_part(
+        CHUNKS[3], spots, me, cycle, arrivals[3], total, jnp.float32, tuple(range(7))
+    )
+    cycle_sum = cycle_part(CHUNKS[3], spots, me, cycle, arrivals[3], total, jnp.bfloat16, (7,))
     apart = lax.axis_size("ja") // 2
     partner = lax.ppermute(cycle_sum, "ja", [(b, b ^ apart) for b in range(2 * apart)])
     return finish(

time: 248 us -> 245 us (0.988)
  waiting for transfers between devices: 104 us -> 100 us
    ppermute x37, waiting for transfers between devices: 73.5 us -> 69.7 us  [shift_ia(): lax.ppermute(value, 'ia', [(i, (i // 2 + steps) % RING * 2 + (i % 2 ^ fli...]
    pallas_call x4 -> x5, Pallas kernels: 16.8 us -> 17.4 us  [cycle_part(): pl.pallas_call(functools.partial(cycle_kernel, chunk, readers), out_shape...]
  transfers between devices with their start and end apart: 53 -> 53, of which waited for: 17 -> 17; matrix products, arithmetic and copies ran while one was open for 0% -> 0% of each run, Pallas kernels for 20% -> 22%
where the time goes in v2:
time: 245 us; the launch traced here: 242 us
  waiting for transfers between devices  100 us (41%)
  starting transfers between devices  62.5 us (26%)
  Pallas kernels  61.5 us (25%)
  local copies, waits for them, and re-layouts  17.3 us (7%)
    ppermute x37, waiting for transfers between devices, shift_ia(): lax.ppermute(value, 'ia', [(i, (i // 2 + steps) % RING * 2 + (i % 2 ^ fli...  69.7 us
    ppermute x37, starting transfers between devices, shift_ia(): lax.ppermute(value, 'ia', [(i, (i // 2 + steps) % RING * 2 + (i % 2 ^ fli...  40.6 us
    pallas_call x4, Pallas kernels, transform(): pl.pallas_call(functools.partial(transform_kernel, chunk, tuple((start fo...  36.3 us
    ppermute x15, starting transfers between devices, shift_ja(): return lax.ppermute(value, AXES, ring_perm(stage, shift))  21.8 us
    ppermute x15, waiting for transfers between devices, shift_ja(): return lax.ppermute(value, AXES, ring_perm(stage, shift))  19.8 us
    pallas_call x5, Pallas kernels, cycle_part(): pl.pallas_call(functools.partial(cycle_kernel, chunk, readers), out_shape...  17.4 us
    unnamed x62, local copies, waits for them, and re-layouts  16.4 us
    ppermute x1, waiting for transfers between devices, update(): lax.ppermute(cycle_sum, 'ja', [(b, b ^ apart) for b in range(2 * apart)])  10.5 us
  transfers between devices with their start and end apart: 53, of which 17 were waited for; matrix products, arithmetic and copies ran while one was open for 0% of the time, Pallas kernels for 22%

profile of v2, /device:TPU:102, one launch (start us, length us, event | category | flops | bytes accessed | tf_op | source)
XLA Modules:
  0.0 242.4 jit_solution(10120571995149473566)
XLA Ops:
  2.1 5.9 %prep.1 = (bf16[8,640,128]{2,1,0:T(8,128)(2,1)}, bf16[1040,512]{1,0:T(8,128)(2,1)S(1)}, bf16[8,128,128]{2,1,0:T(8,128)(2,1)S(1)}, s32[2,128]{1,0:T(2,128)S(1)}) custom-call(s32[8]{0:T(128)S(1)} %copy-done.17, s32[1,256]{1,0:T(1,128)S(1)} %reshape.13.entries, bf16[8,128,128]{2,1,0:T(8,128)(2,1)} %amps.1, bf16[8,512,128]{2,1,0:T(8,128)(2,1)} %bases.1), custom_call_target="tpu_custom_call" | custom-call | bytes 5242880 | tf_op jit(solution)/shard_map/prep/pallas_call | solution.py:282
  8.0 3.0 %collective-permute-start = (bf16[1040,512]{1,0:T(8,128)(2,1)S(1)}, bf16[1040,512]{1,0:T(8,128)(2,1)S(1)}, u32[]{:S(2)}, u32[]{:S(2)}) collective-permute-start(bf16[1040,512]{1,0:T(8,128)(2,1)S(1)} %get-tuple-element.83.refs_0_.refs_4_.refs_5_), channel_id=1, source_target_pairs={{0,96},{16,112},{32,0},{48,16},{64,32},{80,48},{96,64},{112,80},{1... | collective-permute-start | bytes 3194888 | tf_op jit(solution)/shard_map/ppermute | solution.py:42
  11.8 2.4 collective-permute-start.8
  14.2 19.5 %collective-permute-done.refs_1_.refs_6_.refs_7_ = bf16[1040,512]{1,0:T(8,128)(2,1)S(1)} collective-permute-done((bf16[1040,512]{1,0:T(8,128)(2,1)S(1)}, bf16[1040,512]{1,0:T(8,128)(2,1)S(1)}, u32[]{:S(2)}, u32[]{:S(2)}) %collective-permute-start) | collective-permute-done | bytes 1064992 | tf_op jit(solution)/shard_map/ppermute | solution.py:42
  33.8 3.8 %collective-permute-start.1 = (bf16[528,512]{1,0:T(8,128)(2,1)S(1)}, bf16[528,512]{1,0:T(8,128)(2,1)S(1)}, u32[]{:S(2)}, u32[]{:S(2)}) collective-permute-start(bf16[528,512]{1,0:T(8,128)(2,1)S(1)} %slice.8), channel_id=1, source_target_pairs={{0,96},{16,112},{32,0},{48,16},{64,32},{80,48},{96,64},{112,80},{1... | collective-permute-start | bytes 1622024 | tf_op jit(solution)/shard_map/ppermute | solution.py:42
  40.2 11.2 %collective-permute-done.10.refs_8_ = bf16[512,512]{1,0:T(8,128)(2,1)S(1)} collective-permute-done((bf16[512,512]{1,0:T(8,128)(2,1)S(1)}, bf16[512,512]{1,0:T(8,128)(2,1)S(1)}, u32[]{:S(2)}, u32[]{:S(2)}) %collective-permute-start.10) | collective-permute-done | bytes 524320 | tf_op jit(solution)/shard_map/ppermute | solution.py:42
  52.7 2.1 collective-permute-done.11.refs_16_
  61.9 2.8 %collective-permute-start.30 = (bf16[8,640,128]{2,1,0:T(8,128)(2,1)}, bf16[8,640,128]{2,1,0:T(8,128)(2,1)}, u32[]{:S(2)}, u32[]{:S(2)}) collective-permute-start(bf16[8,640,128]{2,1,0:T(8,128)(2,1)} %collective-permute-done.7.refs_1_), channel_id=1, source_target_pairs={{0,1},{1,2},{2,3},{3,0},{4,5},{5,6},{6,7},{7,4},{8,9},{9,10},{10,1... | collective-permute-start | bytes 3932168 | tf_op jit(solution)/shard_map/ppermute | solution.py:37
  67.1 3.5 %collective-permute-start.31 = (bf16[8,640,128]{2,1,0:T(8,128)(2,1)}, bf16[8,640,128]{2,1,0:T(8,128)(2,1)}, u32[]{:S(2)}, u32[]{:S(2)}) collective-permute-start(bf16[8,640,128]{2,1,0:T(8,128)(2,1)} %collective-permute-done.8.refs_2_), channel_id=1, source_target_pairs={{0,3},{1,0},{2,1},{3,2},{4,7},{5,4},{6,5},{7,6},{8,11},{9,8},{10,9... | collective-permute-start | bytes 3932168 | tf_op jit(solution)/shard_map/ppermute | solution.py:37
  79.3 9.6 %transform.4 = (bf16[4,2,128,128]{3,2,1,0:T(8,128)(2,1)S(1)}, bf16[4,2,128,128]{3,2,1,0:T(8,128)(2,1)S(1)}, bf16[4,2,128,128]{3,2,1,0:T(8,128)(2,1)S(1)}, bf16[4...) custom-call(s32[8,128]{1,0:T(8,128)S(1)} %notes.1.codes, ...), custom_call_target="tpu_custom_call" | custom-call | flops 6442450944 | bytes 16777216 | tf_op jit(solution)/shard_map/transform/pallas_call | solution.py:154
  89.0 4.3 %collective-permute-start.13 = (bf16[4,2,128,128]{3,2,1,0:T(8,128)(2,1)S(1)}, bf16[4,2,128,128]{3,2,1,0:T(8,128)(2,1)S(1)}, u32[]{:S(2)}, u32[]{:S(2)}) collective-permute-start(bf16[4,2,128,128]{3,2,1,0:T(8,128)(2,1)S(1)} %get-tuple-element.98), channel_id=1, source_target_pairs={{0,64},{16,80},{32,96},{48,112},{64,0},{80,16},{96,32},{112,48},{1... | collective-permute-start | bytes 786440 | tf_op jit(solution)/shard_map/ppermute | solution.py:42
  96.0 9.9 %collective-permute-done.31.refs_1_ = bf16[8,640,128]{2,1,0:T(8,128)(2,1)} collective-permute-done((bf16[8,640,128]{2,1,0:T(8,128)(2,1)}, bf16[8,640,128]{2,1,0:T(8,128)(2,1)}, u32[]{:S(2)}, u32[]{:S(2)}) %collective-permute-start.31) | collective-permute-done | bytes 1310752 | tf_op jit(solution)/shard_map/ppermute | solution.py:37
  107.4 2.3 collective-permute-start.18
  109.7 2.4 %collective-permute-start.32 = (bf16[8,640,128]{2,1,0:T(8,128)(2,1)S(1)}, bf16[8,640,128]{2,1,0:T(8,128)(2,1)S(1)}, u32[]{:S(2)}, u32[]{:S(2)}) collective-permute-start(bf16[8,640,128]{2,1,0:T(8,128)(2,1)S(1)} %copy-done.23), channel_id=1, source_target_pairs={{0,1},{1,2},{2,3},{3,0},{4,5},{5,6},{6,7},{7,4},{8,9},{9,10},{10,1... | collective-permute-start | bytes 3932168 | tf_op jit(solution)/shard_map/ppermute | solution.py:37
  112.1 9.6 %transform.5 = (bf16[4,2,128,128]{3,2,1,0:T(8,128)(2,1)S(1)}, bf16[4,2,128,128]{3,2,1,0:T(8,128)(2,1)S(1)}, bf16[4,2,128,128]{3,2,1,0:T(8,128)(2,1)S(1)}, bf16[4...) custom-call(s32[8,128]{1,0:T(8,128)S(1)} %notes.1.codes, ...), custom_call_target="tpu_custom_call" | custom-call | flops 6442450944 | bytes 16777216 | tf_op jit(solution)/shard_map/transform/pallas_call | solution.py:154
  125.6 10.4 %collective-permute-done.23.refs_1_ = bf16[4,2,128,128]{3,2,1,0:T(8,128)(2,1)S(1)} collective-permute-done((bf16[4,2,128,128]{3,2,1,0:T(8,128)(2,1)S(1)}, bf16[4,2,128,128]{3,2,1,0:T(8,128)(2,1)S(1)}, u32[]{:S(2)}, u32[]{:S(2)}) %collective-permute-start.23) | collective-permute-done | bytes 262176 | tf_op jit(solution)/shard_map/ppermute | solution.py:42
  139.4 11.4 %collective-permute-done.27.refs_5_ = bf16[4,2,128,128]{3,2,1,0:T(8,128)(2,1)S(1)} collective-permute-done((bf16[4,2,128,128]{3,2,1,0:T(8,128)(2,1)S(1)}, bf16[4,2,128,128]{3,2,1,0:T(8,128)(2,1)S(1)}, u32[]{:S(2)}, u32[]{:S(2)}) %collective-permute-start.27) | collective-permute-done | bytes 262176 | tf_op jit(solution)/shard_map/ppermute | solution.py:42
  150.9 3.1 %collective-permute-start.36 = (bf16[8,640,128]{2,1,0:T(8,128)(2,1)}, bf16[8,640,128]{2,1,0:T(8,128)(2,1)S(1)}, u32[]{:S(2)}, u32[]{:S(2)}) collective-permute-start(bf16[8,640,128]{2,1,0:T(8,128)(2,1)} %collective-permute-done.20.refs_1_), channel_id=1, source_target_pairs={{0,1},{1,2},{2,3},{3,0},{4,5},{5,6},{6,7},{7,4},{8,9},{9,10},{10,1... | collective-permute-start | bytes 3932168 | tf_op jit(solution)/shard_map/ppermute | solution.py:37
  154.1 4.2 %cycle.5.refs_8_ = f32[8,128,128]{2,1,0:T(8,128)S(1)} custom-call(s32[256]{0:T(256)S(1)} %bitcast.11, s32[2]{0:T(128)S(1)} %pad_add_fusion.me, bf16[256,128,128]{2,1,0:T(8,128)(2,1)S(1)} %bitcast.6, bf16[4,2,128,128]{3,2,1,0:T(8,128)(2,1)S(1)} %get-tuple-element.96.refs_0_, bf16[4,2,128,128]{3,2,1,0:T(8,128)(2,1)S(1)} %collective-permute-done.12.refs_1_, ...), custom_call_target="tpu_custom_call" | custom-call | flops 2147483648 | bytes 6291456 | tf_op jit(solution)/shard_map/cycle/pallas_call | solution.py:213
  158.3 9.3 %transform.6 = (bf16[4,2,128,128]{3,2,1,0:T(8,128)(2,1)S(1)}, bf16[4,2,128,128]{3,2,1,0:T(8,128)(2,1)S(1)}, bf16[4,2,128,128]{3,2,1,0:T(8,128)(2,1)S(1)}, bf16[4...) custom-call(s32[8,128]{1,0:T(8,128)S(1)} %notes.1.codes, ...), custom_call_target="tpu_custom_call" | custom-call | flops 6442450944 | bytes 16777216 | tf_op jit(solution)/shard_map/transform/pallas_call | solution.py:154
  167.6 4.2 %cycle.6.refs_8_ = f32[8,128,128]{2,1,0:T(8,128)S(1)} custom-call(s32[256]{0:T(256)S(1)} %bitcast.12, s32[2]{0:T(128)S(1)} %pad_add_fusion.me, bf16[256,128,128]{2,1,0:T(8,128)(2,1)S(1)} %bitcast.7, bf16[4,2,128,128]{3,2,1,0:T(8,128)(2,1)S(1)} %get-tuple-element.115.refs_0_, bf16[4,2,128,128]{3,2,1,0:T(8,128)(2,1)S(1)} %collective-permute-done.23.refs_1_, ...), custom_call_target="tpu_custom_call" | custom-call | flops 2147483648 | bytes 6291456 | tf_op jit(solution)/shard_map/cycle/pallas_call | solution.py:213
  173.9 2.3 collective-permute-start.47
  176.2 7.6 %collective-permute-done.37.refs_3_ = bf16[8,640,128]{2,1,0:T(8,128)(2,1)S(1)} collective-permute-done((bf16[8,640,128]{2,1,0:T(8,128)(2,1)S(1)}, bf16[8,640,128]{2,1,0:T(8,128)(2,1)S(1)}, u32[]{:S(2)}, u32[]{:S(2)}) %collective-permute-start.37) | collective-permute-done | bytes 1310752 | tf_op jit(solution)/shard_map/ppermute | solution.py:37
  183.8 7.9 %transform.7 = (bf16[4,2,128,128]{3,2,1,0:T(8,128)(2,1)S(1)}, bf16[4,2,128,128]{3,2,1,0:T(8,128)(2,1)S(1)}, bf16[4,2,128,128]{3,2,1,0:T(8,128)(2,1)S(1)}, bf16[4...) custom-call(s32[8,128]{1,0:T(8,128)S(1)} %notes.1.codes, ...), custom_call_target="tpu_custom_call" | custom-call | flops 6442450944 | bytes 16777216 | tf_op jit(solution)/shard_map/transform/pallas_call | solution.py:154
  197.1 2.5 %collective-permute-start.41 = (bf16[4,2,128,128]{3,2,1,0:T(8,128)(2,1)S(1)}, bf16[4,2,128,128]{3,2,1,0:T(8,128)(2,1)S(1)}, u32[]{:S(2)}, u32[]{:S(2)}) collective-permute-start(bf16[4,2,128,128]{3,2,1,0:T(8,128)(2,1)S(1)} %get-tuple-element.147), channel_id=1, source_target_pairs={{0,96},{16,112},{32,0},{48,16},{64,32},{80,48},{96,64},{112,80},{1... | collective-permute-start | bytes 786440 | tf_op jit(solution)/shard_map/ppermute | solution.py:42
  199.6 2.4 collective-permute-done.50.refs_6_
  201.9 5.0 %collective-permute-done.51.refs_7_ = bf16[4,2,128,128]{3,2,1,0:T(8,128)(2,1)S(1)} collective-permute-done((bf16[4,2,128,128]{3,2,1,0:T(8,128)(2,1)S(1)}, bf16[4,2,128,128]{3,2,1,0:T(8,128)(2,1)S(1)}, u32[]{:S(2)}, u32[]{:S(2)}) %collective-permute-start.51) | collective-permute-done | bytes 262176 | tf_op jit(solution)/shard_map/ppermute | solution.py:42
  207.7 5.3 %collective-permute-start.44 = (bf16[4,2,128,128]{3,2,1,0:T(8,128)(2,1)S(1)}, bf16[4,2,128,128]{3,2,1,0:T(8,128)(2,1)S(1)}, u32[]{:S(2)}, u32[]{:S(2)}) collective-permute-start(bf16[4,2,128,128]{3,2,1,0:T(8,128)(2,1)S(1)} %get-tuple-element.150), channel_id=1, source_target_pairs={{0,80},{16,64},{32,112},{48,96},{64,16},{80,0},{96,48},{112,32},{1... | collective-permute-start | bytes 786440 | tf_op jit(solution)/shard_map/ppermute | solution.py:42
  214.4 4.2 %cycle.7.refs_7_ = f32[8,128,128]{2,1,0:T(8,128)S(1)} custom-call(s32[256]{0:T(256)S(1)} %bitcast.13, s32[2]{0:T(128)S(1)} %pad_add_fusion.me, bf16[256,128,128]{2,1,0:T(8,128)(2,1)S(1)} %bitcast.8, bf16[4,2,128,128]{3,2,1,0:T(8,128)(2,1)S(1)} %get-tuple-element.151.refs_0_, bf16[4,2,128,128]{3,2,1,0:T(8,128)(2,1)S(1)} %collective-permute-done.45.refs_1_, ...), custom_call_target="tpu_custom_call" | custom-call | flops 2147483648 | bytes 6291456 | tf_op jit(solution)/shard_map/cycle/pallas_call | solution.py:213
  219.7 3.8 %collective-permute-done.44.refs_6_ = bf16[4,2,128,128]{3,2,1,0:T(8,128)(2,1)S(1)} collective-permute-done((bf16[4,2,128,128]{3,2,1,0:T(8,128)(2,1)S(1)}, bf16[4,2,128,128]{3,2,1,0:T(8,128)(2,1)S(1)}, u32[]{:S(2)}, u32[]{:S(2)}) %collective-permute-start.44) | collective-permute-done | bytes 262176 | tf_op jit(solution)/shard_map/ppermute | solution.py:42
  223.4 3.8 %cycle.8.refs_1_ = f32[8,128,128]{2,1,0:T(8,128)S(1)} custom-call(s32[256]{0:T(256)S(1)} %bitcast.14, s32[2]{0:T(128)S(1)} %pad_add_fusion.me, bf16[256,128,128]{2,1,0:T(8,128)(2,1)S(1)} %bitcast.9, bf16[4,2,128,128]{3,2,1,0:T(8,128)(2,1)S(1)} %get-tuple-element.144.refs_0_, bf16[4,2,128,128]{3,2,1,0:T(8,128)(2,1)S(1)} %collective-permute-done.39.refs_1_, ...), custom_call_target="tpu_custom_call" | custom-call | flops 1879048192 | bytes 6291456 | tf_op jit(solution)/shard_map/cycle/pallas_call | solution.py:213
  230.1 10.5 %collective-permute-done.52.partner = bf16[8,128,128]{2,1,0:T(8,128)(2,1)S(1)} collective-permute-done((bf16[8,128,128]{2,1,0:T(8,128)(2,1)S(1)}, bf16[8,128,128]{2,1,0:T(8,128)(2,1)S(1)}, u32[]{:S(2)}, u32[]{:S(2)}) %collective-permute-start.52) | collective-permute-done | bytes 262176 | tf_op jit(solution)/shard_map/ppermute | solution.py:456
  (155 shorter events, 51.3 us)
Async XLA Ops:
  8.0 25.8 %collective-permute-start = (bf16[1040,512]{1,0:T(8,128)(2,1)S(1)}, bf16[1040,512]{1,0:T(8,128)(2,1)S(1)}, u32[]{:S(2)}, u32[]{:S(2)}) collective-permute-start(bf16[1040,512]{1,0:T(8,128)(2,1)S(1)} %get-tuple-element.83.refs_0_.refs_4_.refs_5_), channel_id=1, source_target_pairs={{0,96},{16,112},{32,0},{48,16},{64,32},{80,48},{96,64},{112,80},{1... | collective-permute-start | bytes 3194888 | tf_op jit(solution)/shard_map/ppermute | solution.py:42
  11.0 26.6 %collective-permute-start.2 = (bf16[1040,512]{1,0:T(8,128)(2,1)S(1)}, bf16[1040,512]{1,0:T(8,128)(2,1)S(1)}, u32[]{:S(2)}, u32[]{:S(2)}) collective-permute-start(bf16[1040,512]{1,0:T(8,128)(2,1)S(1)} %get-tuple-element.83.refs_0_.refs_4_.refs_5_), channel_id=1, source_target_pairs={{0,32},{16,48},{32,64},{48,80},{64,96},{80,112},{96,0},{112,16},{1... | collective-permute-start | bytes 3194888 | tf_op jit(solution)/shard_map/ppermute | solution.py:42
  11.0 26.7 %collective-permute-start.7 = (bf16[8,640,128]{2,1,0:T(8,128)(2,1)}, bf16[8,640,128]{2,1,0:T(8,128)(2,1)}, u32[]{:S(2)}, u32[]{:S(2)}) collective-permute-start(bf16[8,640,128]{2,1,0:T(8,128)(2,1)} %get-tuple-element.87.refs_0_), channel_id=1, source_target_pairs={{0,12},{1,13},{2,14},{3,15},{4,0},{5,1},{6,2},{7,3},{8,4},{9,5},{1... | collective-permute-start | bytes 3932168 | tf_op jit(solution)/shard_map/ppermute | solution.py:37
  11.8 25.9 %collective-permute-start.8 = (bf16[8,640,128]{2,1,0:T(8,128)(2,1)}, bf16[8,640,128]{2,1,0:T(8,128)(2,1)}, u32[]{:S(2)}, u32[]{:S(2)}) collective-permute-start(bf16[8,640,128]{2,1,0:T(8,128)(2,1)} %get-tuple-element.87.refs_0_), channel_id=1, source_target_pairs={{0,4},{1,5},{2,6},{3,7},{4,8},{5,9},{6,10},{7,11},{8,12},{9,13},{1... | collective-permute-start | bytes 3932168 | tf_op jit(solution)/shard_map/ppermute | solution.py:37
  14.2 25.0 %collective-permute-start.3 = (bf16[1040,512]{1,0:T(8,128)(2,1)S(1)}, bf16[1040,512]{1,0:T(8,128)(2,1)S(1)}, u32[]{:S(2)}, u32[]{:S(2)}) collective-permute-start(bf16[1040,512]{1,0:T(8,128)(2,1)S(1)} %get-tuple-element.83.refs_0_.refs_4_.refs_5_), channel_id=1, source_target_pairs={{0,16},{16,0},{32,48},{48,32},{64,80},{80,64},{96,112},{112,96},{1... | collective-permute-start | bytes 3194888 | tf_op jit(solution)/shard_map/ppermute | solution.py:42
  33.8 17.6 %collective-permute-start.1 = (bf16[528,512]{1,0:T(8,128)(2,1)S(1)}, bf16[528,512]{1,0:T(8,128)(2,1)S(1)}, u32[]{:S(2)}, u32[]{:S(2)}) collective-permute-start(bf16[528,512]{1,0:T(8,128)(2,1)S(1)} %slice.8), channel_id=1, source_target_pairs={{0,96},{16,112},{32,0},{48,16},{64,32},{80,48},{96,64},{112,80},{1... | collective-permute-start | bytes 1622024 | tf_op jit(solution)/shard_map/ppermute | solution.py:42
  37.7 24.2 %collective-permute-start.22 = (bf16[8,640,128]{2,1,0:T(8,128)(2,1)}, bf16[8,640,128]{2,1,0:T(8,128)(2,1)S(1)}, u32[]{:S(2)}, u32[]{:S(2)}) collective-permute-start(bf16[8,640,128]{2,1,0:T(8,128)(2,1)} %get-tuple-element.87.refs_0_), channel_id=1, source_target_pairs={{0,8},{1,9},{2,10},{3,11},{4,12},{5,13},{6,14},{7,15},{8,0},{9,1},... | collective-permute-start | bytes 3932168 | tf_op jit(solution)/shard_map/ppermute | solution.py:37
  39.2 26.8 %collective-permute-start.9 = (bf16[8,640,128]{2,1,0:T(8,128)(2,1)}, bf16[8,640,128]{2,1,0:T(8,128)(2,1)S(1)}, u32[]{:S(2)}, u32[]{:S(2)}) collective-permute-start(bf16[8,640,128]{2,1,0:T(8,128)(2,1)} %get-tuple-element.87.refs_0_), channel_id=1, source_target_pairs={{0,1},{1,2},{2,3},{3,0},{4,5},{5,6},{6,7},{7,4},{8,9},{9,10},{10,1... | collective-permute-start | bytes 3932168 | tf_op jit(solution)/shard_map/ppermute | solution.py:37
  40.2 16.4 %collective-permute-start.4 = (bf16[1040,512]{1,0:T(8,128)(2,1)S(1)}, bf16[1040,512]{1,0:T(8,128)(2,1)S(1)}, u32[]{:S(2)}, u32[]{:S(2)}) collective-permute-start(bf16[1040,512]{1,0:T(8,128)(2,1)S(1)} %collective-permute-done.refs_1_.refs_6_.refs_7_), channel_id=1, source_target_pairs={{0,16},{16,0},{32,48},{48,32},{64,80},{80,64},{96,112},{112,96},{1... | collective-permute-start | bytes 3194888 | tf_op jit(solution)/shard_map/ppermute | solution.py:42
  57.6 31.3 %collective-permute-start.20 = (bf16[8,640,128]{2,1,0:T(8,128)(2,1)}, bf16[8,640,128]{2,1,0:T(8,128)(2,1)}, u32[]{:S(2)}, u32[]{:S(2)}) collective-permute-start(bf16[8,640,128]{2,1,0:T(8,128)(2,1)} %collective-permute-done.8.refs_2_), channel_id=1, source_target_pairs={{0,1},{1,2},{2,3},{3,0},{4,5},{5,6},{6,7},{7,4},{8,9},{9,10},{10,1... | collective-permute-start | bytes 3932168 | tf_op jit(solution)/shard_map/ppermute | solution.py:37
  58.6 30.4 %collective-permute-start.21 = (bf16[8,640,128]{2,1,0:T(8,128)(2,1)}, bf16[8,640,128]{2,1,0:T(8,128)(2,1)}, u32[]{:S(2)}, u32[]{:S(2)}) collective-permute-start(bf16[8,640,128]{2,1,0:T(8,128)(2,1)} %collective-permute-done.7.refs_1_), channel_id=1, source_target_pairs={{0,3},{1,0},{2,1},{3,2},{4,7},{5,4},{6,5},{7,6},{8,11},{9,8},{10,9... | collective-permute-start | bytes 3932168 | tf_op jit(solution)/shard_map/ppermute | solution.py:37
  61.5 31.8 %collective-permute-start.19 = (bf16[8,640,128]{2,1,0:T(8,128)(2,1)}, bf16[8,640,128]{2,1,0:T(8,128)(2,1)}, u32[]{:S(2)}, u32[]{:S(2)}) collective-permute-start(bf16[8,640,128]{2,1,0:T(8,128)(2,1)} %get-tuple-element.87.refs_0_), channel_id=1, source_target_pairs={{0,3},{1,0},{2,1},{3,2},{4,7},{5,4},{6,5},{7,6},{8,11},{9,8},{10,9... | collective-permute-start | bytes 3932168 | tf_op jit(solution)/shard_map/ppermute | solution.py:37
  61.9 32.4 %collective-permute-start.30 = (bf16[8,640,128]{2,1,0:T(8,128)(2,1)}, bf16[8,640,128]{2,1,0:T(8,128)(2,1)}, u32[]{:S(2)}, u32[]{:S(2)}) collective-permute-start(bf16[8,640,128]{2,1,0:T(8,128)(2,1)} %collective-permute-done.7.refs_1_), channel_id=1, source_target_pairs={{0,1},{1,2},{2,3},{3,0},{4,5},{5,6},{6,7},{7,4},{8,9},{9,10},{10,1... | collective-permute-start | bytes 3932168 | tf_op jit(solution)/shard_map/ppermute | solution.py:37
  67.1 38.7 %collective-permute-start.31 = (bf16[8,640,128]{2,1,0:T(8,128)(2,1)}, bf16[8,640,128]{2,1,0:T(8,128)(2,1)}, u32[]{:S(2)}, u32[]{:S(2)}) collective-permute-start(bf16[8,640,128]{2,1,0:T(8,128)(2,1)} %collective-permute-done.8.refs_2_), channel_id=1, source_target_pairs={{0,3},{1,0},{2,1},{3,2},{4,7},{5,4},{6,5},{7,6},{8,11},{9,8},{10,9... | collective-permute-start | bytes 3932168 | tf_op jit(solution)/shard_map/ppermute | solution.py:37
  88.9 17.7 %collective-permute-start.12 = (bf16[4,2,128,128]{3,2,1,0:T(8,128)(2,1)S(1)}, bf16[4,2,128,128]{3,2,1,0:T(8,128)(2,1)S(1)}, u32[]{:S(2)}, u32[]{:S(2)}) collective-permute-start(bf16[4,2,128,128]{3,2,1,0:T(8,128)(2,1)S(1)} %get-tuple-element.97), channel_id=1, source_target_pairs={{0,32},{16,48},{32,64},{48,80},{64,96},{80,112},{96,0},{112,16},{1... | collective-permute-start | bytes 786440 | tf_op jit(solution)/shard_map/ppermute | solution.py:42
  89.0 17.6 %collective-permute-start.13 = (bf16[4,2,128,128]{3,2,1,0:T(8,128)(2,1)S(1)}, bf16[4,2,128,128]{3,2,1,0:T(8,128)(2,1)S(1)}, u32[]{:S(2)}, u32[]{:S(2)}) collective-permute-start(bf16[4,2,128,128]{3,2,1,0:T(8,128)(2,1)S(1)} %get-tuple-element.98), channel_id=1, source_target_pairs={{0,64},{16,80},{32,96},{48,112},{64,0},{80,16},{96,32},{112,48},{1... | collective-permute-start | bytes 786440 | tf_op jit(solution)/shard_map/ppermute | solution.py:42
  105.8 48.2 %collective-permute-start.33 = (bf16[8,640,128]{2,1,0:T(8,128)(2,1)S(1)}, bf16[8,640,128]{2,1,0:T(8,128)(2,1)S(1)}, u32[]{:S(2)}, u32[]{:S(2)}) collective-permute-start(bf16[8,640,128]{2,1,0:T(8,128)(2,1)S(1)} %copy-done.23), channel_id=1, source_target_pairs={{0,3},{1,0},{2,1},{3,2},{4,7},{5,4},{6,5},{7,6},{8,11},{9,8},{10,9... | collective-permute-start | bytes 3932168 | tf_op jit(solution)/shard_map/ppermute | solution.py:37
  106.7 16.2 %collective-permute-start.17 = (bf16[4,2,128,128]{3,2,1,0:T(8,128)(2,1)S(1)}, bf16[4,2,128,128]{3,2,1,0:T(8,128)(2,1)S(1)}, u32[]{:S(2)}, u32[]{:S(2)}) collective-permute-start(bf16[4,2,128,128]{3,2,1,0:T(8,128)(2,1)S(1)} %get-tuple-element.102), channel_id=1, source_target_pairs={{0,80},{16,64},{32,112},{48,96},{64,16},{80,0},{96,48},{112,32},{1... | collective-permute-start | bytes 786440 | tf_op jit(solution)/shard_map/ppermute | solution.py:42
  107.4 16.8 %collective-permute-start.18 = (bf16[4,2,128,128]{3,2,1,0:T(8,128)(2,1)S(1)}, bf16[4,2,128,128]{3,2,1,0:T(8,128)(2,1)S(1)}, u32[]{:S(2)}, u32[]{:S(2)}) collective-permute-start(bf16[4,2,128,128]{3,2,1,0:T(8,128)(2,1)S(1)} %get-tuple-element.103), channel_id=1, source_target_pairs={{0,112},{16,96},{32,16},{48,0},{64,48},{80,32},{96,80},{112,64},{1... | collective-permute-start | bytes 786440 | tf_op jit(solution)/shard_map/ppermute | solution.py:42
  109.7 48.5 %collective-permute-start.32 = (bf16[8,640,128]{2,1,0:T(8,128)(2,1)S(1)}, bf16[8,640,128]{2,1,0:T(8,128)(2,1)S(1)}, u32[]{:S(2)}, u32[]{:S(2)}) collective-permute-start(bf16[8,640,128]{2,1,0:T(8,128)(2,1)S(1)} %copy-done.23), channel_id=1, source_target_pairs={{0,1},{1,2},{2,3},{3,0},{4,5},{5,6},{6,7},{7,4},{8,9},{9,10},{10,1... | collective-permute-start | bytes 3932168 | tf_op jit(solution)/shard_map/ppermute | solution.py:37
  137.5 35.9 %collective-permute-start.34 = (bf16[8,640,128]{2,1,0:T(8,128)(2,1)S(1)}, bf16[8,640,128]{2,1,0:T(8,128)(2,1)S(1)}, u32[]{:S(2)}, u32[]{:S(2)}) collective-permute-start(bf16[8,640,128]{2,1,0:T(8,128)(2,1)S(1)} %copy-done.21), channel_id=1, source_target_pairs={{0,1},{1,2},{2,3},{3,0},{4,5},{5,6},{6,7},{7,4},{8,9},{9,10},{10,1... | collective-permute-start | bytes 3932168 | tf_op jit(solution)/shard_map/ppermute | solution.py:37
  150.8 23.1 %collective-permute-start.35 = (bf16[8,640,128]{2,1,0:T(8,128)(2,1)}, bf16[8,640,128]{2,1,0:T(8,128)(2,1)S(1)}, u32[]{:S(2)}, u32[]{:S(2)}) collective-permute-start(bf16[8,640,128]{2,1,0:T(8,128)(2,1)} %collective-permute-done.21.refs_2_), channel_id=1, source_target_pairs={{0,3},{1,0},{2,1},{3,2},{4,7},{5,4},{6,5},{7,6},{8,11},{9,8},{10,9... | collective-permute-start | bytes 3932168 | tf_op jit(solution)/shard_map/ppermute | solution.py:37
  150.9 25.3 %collective-permute-start.36 = (bf16[8,640,128]{2,1,0:T(8,128)(2,1)}, bf16[8,640,128]{2,1,0:T(8,128)(2,1)S(1)}, u32[]{:S(2)}, u32[]{:S(2)}) collective-permute-start(bf16[8,640,128]{2,1,0:T(8,128)(2,1)} %collective-permute-done.20.refs_1_), channel_id=1, source_target_pairs={{0,1},{1,2},{2,3},{3,0},{4,5},{5,6},{6,7},{7,4},{8,9},{9,10},{10,1... | collective-permute-start | bytes 3932168 | tf_op jit(solution)/shard_map/ppermute | solution.py:37
  154.0 29.8 %collective-permute-start.37 = (bf16[8,640,128]{2,1,0:T(8,128)(2,1)S(1)}, bf16[8,640,128]{2,1,0:T(8,128)(2,1)S(1)}, u32[]{:S(2)}, u32[]{:S(2)}) collective-permute-start(bf16[8,640,128]{2,1,0:T(8,128)(2,1)S(1)} %collective-permute-done.33.refs_3_), channel_id=1, source_target_pairs={{0,3},{1,0},{2,1},{3,2},{4,7},{5,4},{6,5},{7,6},{8,11},{9,8},{10,9... | collective-permute-start | bytes 3932168 | tf_op jit(solution)/shard_map/ppermute | solution.py:37
  171.8 19.9 %collective-permute-start.45 = (bf16[4,2,128,128]{3,2,1,0:T(8,128)(2,1)S(1)}, bf16[4,2,128,128]{3,2,1,0:T(8,128)(2,1)S(1)}, u32[]{:S(2)}, u32[]{:S(2)}) collective-permute-start(bf16[4,2,128,128]{3,2,1,0:T(8,128)(2,1)S(1)} %get-tuple-element.152), channel_id=1, source_target_pairs={{0,32},{16,48},{32,64},{48,80},{64,96},{80,112},{96,0},{112,16},{1... | collective-permute-start | bytes 786440 | tf_op jit(solution)/shard_map/ppermute | solution.py:42
  173.4 19.8 %collective-permute-start.46 = (bf16[4,2,128,128]{3,2,1,0:T(8,128)(2,1)S(1)}, bf16[4,2,128,128]{3,2,1,0:T(8,128)(2,1)S(1)}, u32[]{:S(2)}, u32[]{:S(2)}) collective-permute-start(bf16[4,2,128,128]{3,2,1,0:T(8,128)(2,1)S(1)} %get-tuple-element.153), channel_id=1, source_target_pairs={{0,64},{16,80},{32,96},{48,112},{64,0},{80,16},{96,32},{112,48},{1... | collective-permute-start | bytes 786440 | tf_op jit(solution)/shard_map/ppermute | solution.py:42
  173.9 21.0 %collective-permute-start.47 = (bf16[4,2,128,128]{3,2,1,0:T(8,128)(2,1)S(1)}, bf16[4,2,128,128]{3,2,1,0:T(8,128)(2,1)S(1)}, u32[]{:S(2)}, u32[]{:S(2)}) collective-permute-start(bf16[4,2,128,128]{3,2,1,0:T(8,128)(2,1)S(1)} %get-tuple-element.154), channel_id=1, source_target_pairs={{0,96},{16,112},{32,0},{48,16},{64,32},{80,48},{96,64},{112,80},{1... | collective-permute-start | bytes 786440 | tf_op jit(solution)/shard_map/ppermute | solution.py:42
  176.2 19.5 %collective-permute-start.48 = (bf16[4,2,128,128]{3,2,1,0:T(8,128)(2,1)S(1)}, bf16[4,2,128,128]{3,2,1,0:T(8,128)(2,1)S(1)}, u32[]{:S(2)}, u32[]{:S(2)}) collective-permute-start(bf16[4,2,128,128]{3,2,1,0:T(8,128)(2,1)S(1)} %get-tuple-element.155), channel_id=1, source_target_pairs={{0,16},{16,0},{32,48},{48,32},{64,80},{80,64},{96,112},{112,96},{1... | collective-permute-start | bytes 786440 | tf_op jit(solution)/shard_map/ppermute | solution.py:42
  195.7 17.3 %collective-permute-start.40 = (bf16[4,2,128,128]{3,2,1,0:T(8,128)(2,1)S(1)}, bf16[4,2,128,128]{3,2,1,0:T(8,128)(2,1)S(1)}, u32[]{:S(2)}, u32[]{:S(2)}) collective-permute-start(bf16[4,2,128,128]{3,2,1,0:T(8,128)(2,1)S(1)} %get-tuple-element.146), channel_id=1, source_target_pairs={{0,64},{16,80},{32,96},{48,112},{64,0},{80,16},{96,32},{112,48},{1... | collective-permute-start | bytes 786440 | tf_op jit(solution)/shard_map/ppermute | solution.py:42
  197.1 22.6 %collective-permute-start.41 = (bf16[4,2,128,128]{3,2,1,0:T(8,128)(2,1)S(1)}, bf16[4,2,128,128]{3,2,1,0:T(8,128)(2,1)S(1)}, u32[]{:S(2)}, u32[]{:S(2)}) collective-permute-start(bf16[4,2,128,128]{3,2,1,0:T(8,128)(2,1)S(1)} %get-tuple-element.147), channel_id=1, source_target_pairs={{0,96},{16,112},{32,0},{48,16},{64,32},{80,48},{96,64},{112,80},{1... | collective-permute-start | bytes 786440 | tf_op jit(solution)/shard_map/ppermute | solution.py:42
  201.9 17.7 %collective-permute-start.42 = (bf16[4,2,128,128]{3,2,1,0:T(8,128)(2,1)S(1)}, bf16[4,2,128,128]{3,2,1,0:T(8,128)(2,1)S(1)}, u32[]{:S(2)}, u32[]{:S(2)}) collective-permute-start(bf16[4,2,128,128]{3,2,1,0:T(8,128)(2,1)S(1)} %get-tuple-element.148), channel_id=1, source_target_pairs={{0,16},{16,0},{32,48},{48,32},{64,80},{80,64},{96,112},{112,96},{1... | collective-permute-start | bytes 786440 | tf_op jit(solution)/shard_map/ppermute | solution.py:42
  213.0 16.0 %collective-permute-start.38 = (bf16[4,2,128,128]{3,2,1,0:T(8,128)(2,1)S(1)}, bf16[4,2,128,128]{3,2,1,0:T(8,128)(2,1)S(1)}, u32[]{:S(2)}, u32[]{:S(2)}) collective-permute-start(bf16[4,2,128,128]{3,2,1,0:T(8,128)(2,1)S(1)} %get-tuple-element.143), channel_id=1, source_target_pairs={{0,112},{16,96},{32,16},{48,0},{64,48},{80,32},{96,80},{112,64},{1... | collective-permute-start | bytes 786440 | tf_op jit(solution)/shard_map/ppermute | solution.py:42
  (52 other events, 490.1 us)
